TPU v7x, 32 devices: a whole 2x2x4 slice. The times are simulated.
32 devices in a mesh: gx: 4 (over z), gy: 4 (over y, core), col: 2 (over x).
Axes of the slice: x: 2, y: 2, z: 4, core: 2. Of those that a mesh axis runs over, the one named last changes fastest.
Arguments:
- sources: float32 [4, 4, 2, 128, 1152], P('gx', 'gy', None, 'col'), may hold values from -100 to 100
- impedance: bfloat16 [4, 4, 2, 1152, 1152], P('gx', 'gy'), may hold values from -0.09375 to 0.09375
- pair_maps: bfloat16 [4, 4, 2, 2, 384, 384], P('gx', 'gy'), may hold values from -0.21875 to 0.21875
- lead_side: int32 [4, 4, 2], P('gx', 'gy'), may hold values from 0 to 1
- coarse_basis: float32 [4, 4, 32, 2, 1152], P('gx', 'gy'), may hold values from -0.125 to 0.125
- coarse_inverse: float32 [512, 512], P(('gx', 'gy', 'col')), may hold values from -0.6 to 0.6
Outputs:
- solution_traces: float32 [4, 4, 2, 128, 1152], P('gx', 'gy', None, 'col')
Inputs may be any that keep to these rules, and one draw needn't show every extreme that they name: `lead_side`: entries of interfaces beyond the last subdomain along a dimension are read by no step.
All inputs are finite; a program needn't handle non-finite values.
Results may differ from a plain program's by a relative error of at most 0.0039.
Values may be sent and summed in bfloat16 or wider, within the bound.
No kernel may reach another device: no remote copies, remote signals or barrier semaphores. Data moves between devices by JAX's collectives and lax.ppermute only.
A program may use at most 64 MiB of HBM per device.

v0:
```python
import jax
import jax.numpy as jnp
from jax import lax
from jax.sharding import PartitionSpec as P

ITERS = 2


STEP_RATIO = 0.4


def shifted(block, axis, distance):
    devices = range(lax.axis_size(axis))
    route = [(i - distance, i) for i in devices if i - distance in devices]
    return lax.ppermute(block, axis, route)


def complex_apply(traces, real_part, imag_part):
    sources_here = traces.shape[1]
    flattened = traces.reshape(2 * sources_here, traces.shape[2])
    first_part = jnp.dot(flattened, real_part, preferred_element_type=jnp.float32).reshape(
        2, sources_here, -1
    )
    second_part = jnp.dot(flattened, imag_part, preferred_element_type=jnp.float32).reshape(
        2, sources_here, -1
    )
    return jnp.stack([first_part[0] - second_part[1], second_part[0] + first_part[1]])


def pair_solve(lower_side, upper_side, solver):
    return complex_apply(jnp.concatenate([lower_side, upper_side], axis=2), solver[0], solver[1])


def orient(solver, leading, face_width):
    swapped = jnp.roll(solver, (face_width, face_width), axis=(1, 2))
    return jnp.where(leading == 0, solver, swapped)


def per_device(sources, impedance, pair_maps, lead_side, coarse_basis, coarse_inverse):
    drive_traces = sources[0, 0]
    sources_here = drive_traces.shape[1]
    face_width = drive_traces.shape[2] // 6
    map_real = impedance[0, 0, 0]
    map_imag = impedance[0, 0, 1]
    basis_here = coarse_basis[0, 0]
    coarse_count = basis_here.shape[0]
    first_count = lax.axis_size("gx")
    second_count = lax.axis_size("gy")
    first_index = lax.axis_index("gx")
    second_index = lax.axis_index("gy")
    first_solver = orient(pair_maps[0, 0, 0], lead_side[0, 0, 0], face_width)
    second_solver = orient(pair_maps[0, 0, 1], lead_side[0, 0, 1], face_width)
    pair_rows = lax.all_gather(coarse_inverse, "col", axis=0, tiled=True)
    row_blocks = pair_rows.reshape(coarse_count, -1, coarse_count)
    iterate = jnp.zeros(drive_traces.shape, jnp.float32)
    for repeat in range(ITERS):
        rounded = iterate.astype(jnp.bfloat16)
        outgoing = (complex_apply(rounded, map_real, map_imag) + drive_traces).astype(jnp.bfloat16)
        first_faces = outgoing[:, :, : 2 * face_width].reshape(2, sources_here, 2, face_width)
        second_faces = outgoing[:, :, 2 * face_width : 4 * face_width].reshape(
            2, sources_here, 2, face_width
        )
        first_above = shifted(first_faces[:, :, 0], "gx", -1)
        second_above = shifted(second_faces[:, :, 0], "gy", -1)
        first_solved = pair_solve(first_faces[:, :, 1], first_above, first_solver)
        second_solved = pair_solve(second_faces[:, :, 1], second_above, second_solver)
        face_one = first_solved[:, :, :face_width]
        face_three = second_solved[:, :, :face_width]
        face_zero = shifted(first_solved[:, :, face_width:], "gx", 1)
        face_two = shifted(second_solved[:, :, face_width:], "gy", 1)
        face_one = jnp.where(first_index < first_count - 1, face_one, 0.0)
        face_three = jnp.where(second_index < second_count - 1, face_three, 0.0)
        updated = jnp.concatenate(
            [
                face_zero,
                face_one,
                face_two,
                face_three,
                outgoing[:, :, 5 * face_width :].astype(jnp.float32),
                outgoing[:, :, 4 * face_width : 5 * face_width].astype(jnp.float32),
            ],
            axis=2,
        )
        defect = updated - iterate
        projected = jnp.einsum("csk,pck->sp", defect, basis_here, precision=lax.Precision.HIGHEST)
        gathered = lax.all_gather(projected[None], ("gx", "gy"), axis=0, tiled=True)
        coarse = jnp.einsum("nsp,qnp->sq", gathered, row_blocks, precision=lax.Precision.HIGHEST)
        correction = jnp.einsum("sp,pck->csk", coarse, basis_here, precision=lax.Precision.HIGHEST)
        defect_norm, correction_norm = lax.psum(
            (jnp.sum(defect * defect, axis=(0, 2)), jnp.sum(correction * correction, axis=(0, 2))),
            ("gx", "gy"),
        )
        factor = STEP_RATIO * jnp.sqrt(defect_norm / (correction_norm + 1e-06))
        iterate = updated + factor[None, :, None] * correction
    return iterate[None, None]


def solution(mesh):
    return jax.shard_map(
        per_device,
        mesh=mesh,
        in_specs=(
            P("gx", "gy", None, "col", None),
            P("gx", "gy", None, None, None),
            P("gx", "gy", None, None, None, None),
            P("gx", "gy", None),
            P("gx", "gy", None, None, None),
            P(("gx", "gy", "col"), None),
        ),
        out_specs=P("gx", "gy", None, "col", None),
        check_vma=False,
    )
```

profile of v0, /device:TPU:0, one launch (start us, length us, event | category | flops | bytes accessed | tf_op | source)
XLA Modules:
  0.0 154.8 jit_solution(12876421462017243072)
XLA Ops:
  0.0 2.4 %fusion.2 = f32[128,1152]{1,0:T(8,128)S(1)} fusion(bf16[1,1,2,1152,1152]{4,3,2,1,0:T(8,128)(2,1)} %param.7), kind=kOutput, calls=%fused_computation.2 | convolution fusion | flops 339738624 | bytes 3244032 | tf_op jit(solution)/shard_map/dot_general | solution.py:24
  2.4 2.4 %fusion.6 = f32[128,1152]{1,0:T(8,128)S(1)} fusion(bf16[1,1,2,1152,1152]{4,3,2,1,0:T(8,128)(2,1)} %param.7), kind=kOutput, calls=%fused_computation.6 | convolution fusion | flops 339738624 | bytes 3244032 | tf_op jit(solution)/shard_map/dot_general | solution.py:21
  5.1 0.8 fusion.79
  6.0 1.3 collective-permute-start.2
  7.6 1.3 collective-permute-start
  12.7 2.4 %collective-permute-done = bf16[2,64,192]{2,1,0:T(8,128)(2,1)S(1)} collective-permute-done((bf16[2,64,192]{2,1,0:T(8,128)(2,1)S(1)}, bf16[2,64,192]{2,1,0:T(8,128)(2,1)S(1)}, u32[]{:S(2)}, u32[]{:S(2)}) %collective-permute-start) | collective-permute-done | bytes 49184 | tf_op jit(solution)/shard_map/ppermute | solution.py:15
  15.8 2.2 %collective-permute-start.3 = (f32[2,64,192]{2,1,0:T(8,128)S(1)}, f32[2,64,192]{2,1,0:T(8,128)S(1)}, u32[]{:S(2)}, u32[]{:S(2)}) collective-permute-start(f32[2,64,192]{2,1,0:T(8,128)S(1)} %get-tuple-element.44), channel_id=1, source_target_pairs={{0,2},{2,4},{4,6},{1,3},{3,5},{5,7},{8,10},{10,12},{12,14},{9,11},... | collective-permute-start | bytes 294920 | tf_op jit(solution)/shard_map/ppermute | solution.py:15
  18.1 4.1 %collective-permute-start.1 = (f32[2,64,192]{2,1,0:T(8,128)S(1)}, f32[2,64,192]{2,1,0:T(8,128)S(1)}, u32[]{:S(2)}, u32[]{:S(2)}) collective-permute-start(f32[2,64,192]{2,1,0:T(8,128)S(1)} %get-tuple-element.46), channel_id=1, source_target_pairs={{0,8},{8,16},{16,24},{1,9},{9,17},{17,25},{2,10},{10,18},{18,26},{... | collective-permute-start | bytes 294920 | tf_op jit(solution)/shard_map/ppermute | solution.py:15
  22.3 4.6 %all_gather.10 = f32[32,512]{1,0:T(8,128)S(1)} all-gather(f32[16,512]{1,0:T(8,128)S(1)} %copy-done.5), channel_id=1, replica_groups=mesh['gx'=4,'gy'=4,'col'=2] {'col'}, dimensions={0}, use_global_device_ids=true | all-gather | bytes 98304 | tf_op jit(solution)/shard_map/all_gather | solution.py:53
  28.0 21.0 %all-gather.2 = f32[16,64,32]{1,2,0:T(8,128)S(1)} all-gather(f32[1,64,32]{1,2,0:T(8,128)S(1)} %convolution_bitcast_fusion.1), channel_id=2, replica_groups=mesh['gx'=4,'gy'=4,'col'=2] {'gx','gy'}, dimensions={0}, use_global_device_ids=true | all-gather | bytes 139264 | tf_op jit(solution)/shard_map/all_gather | solution.py:86
  49.6 0.8 multiply_reduce_fusion.2
  50.4 29.8 %all-reduce.1 = (f32[64]{0:T(128)S(1)}, f32[64]{0:T(128)S(1)}) all-reduce(f32[64]{0:T(128)S(1)} %multiply_reduce_fusion.3, f32[64]{0:T(128)S(1)} %get-tuple-element.57), channel_id=1, replica_groups=mesh['gx'=4,'gy'=4,'col'=2] {'gx','gy'}, use_global_device_ids=true, to_apply=%region_1.2 | all-reduce | flops 128 | bytes 1024 | tf_op jit(solution)/shard_map/psum | solution.py:89
  80.4 2.3 %fusion = f32[128,1152]{1,0:T(8,128)S(1)} fusion(bf16[128,1152]{1,0:T(8,128)(2,1)S(1)} %bitcast.121, bf16[1,1,2,1152,1152]{4,3,2,1,0:T(8,128)(2,1)} %param.7), kind=kOutput, calls=%fused_computation | convolution fusion | flops 339738624 | bytes 3538944 | tf_op jit(solution)/shard_map/dot_general | solution.py:24
  82.7 2.4 %fusion.4 = f32[128,1152]{1,0:T(8,128)S(1)} fusion(bf16[128,1152]{1,0:T(8,128)(2,1)S(1)} %bitcast.122, bf16[1,1,2,1152,1152]{4,3,2,1,0:T(8,128)(2,1)} %param.7), kind=kOutput, calls=%fused_computation.4 | convolution fusion | flops 339738624 | bytes 3538944 | tf_op jit(solution)/shard_map/dot_general | solution.py:21
  85.6 1.3 collective-permute-start.6
  87.3 1.3 collective-permute-start.4
  89.3 4.7 %collective-permute-done.4 = bf16[2,64,192]{2,1,0:T(8,128)(2,1)S(1)} collective-permute-done((bf16[2,64,192]{2,1,0:T(8,128)(2,1)S(1)}, bf16[2,64,192]{2,1,0:T(8,128)(2,1)S(1)}, u32[]{:S(2)}, u32[]{:S(2)}) %collective-permute-start.4) | collective-permute-done | bytes 49184 | tf_op jit(solution)/shard_map/ppermute | solution.py:15
  94.7 2.0 %collective-permute-start.7 = (f32[2,64,192]{2,1,0:T(8,128)S(1)}, f32[2,64,192]{2,1,0:T(8,128)S(1)}, u32[]{:S(2)}, u32[]{:S(2)}) collective-permute-start(f32[2,64,192]{2,1,0:T(8,128)S(1)} %get-tuple-element.40), channel_id=1, source_target_pairs={{0,2},{2,4},{4,6},{1,3},{3,5},{5,7},{8,10},{10,12},{12,14},{9,11},... | collective-permute-start | bytes 294920 | tf_op jit(solution)/shard_map/ppermute | solution.py:15
  96.9 1.7 %collective-permute-start.5 = (f32[2,64,192]{2,1,0:T(8,128)S(1)}, f32[2,64,192]{2,1,0:T(8,128)S(1)}, u32[]{:S(2)}, u32[]{:S(2)}) collective-permute-start(f32[2,64,192]{2,1,0:T(8,128)S(1)} %get-tuple-element.42), channel_id=1, source_target_pairs={{0,8},{8,16},{16,24},{1,9},{9,17},{17,25},{2,10},{10,18},{18,26},{... | collective-permute-start | bytes 294920 | tf_op jit(solution)/shard_map/ppermute | solution.py:15
  98.6 3.6 %collective-permute-done.5 = f32[2,64,192]{2,1,0:T(8,128)S(1)} collective-permute-done((f32[2,64,192]{2,1,0:T(8,128)S(1)}, f32[2,64,192]{2,1,0:T(8,128)S(1)}, u32[]{:S(2)}, u32[]{:S(2)}) %collective-permute-start.5) | collective-permute-done | bytes 98336 | tf_op jit(solution)/shard_map/ppermute | solution.py:15
  103.2 18.1 %all-gather.3 = f32[16,64,32]{1,2,0:T(8,128)S(1)} all-gather(f32[1,64,32]{1,2,0:T(8,128)S(1)} %convolution_bitcast_fusion), channel_id=3, replica_groups=mesh['gx'=4,'gy'=4,'col'=2] {'gx','gy'}, dimensions={0}, use_global_device_ids=true | all-gather | bytes 139264 | tf_op jit(solution)/shard_map/all_gather | solution.py:86
  121.9 0.8 multiply_reduce_fusion
  122.7 31.2 %all-reduce = (f32[64]{0:T(128)S(1)}, f32[64]{0:T(128)S(1)}) all-reduce(f32[64]{0:T(128)S(1)} %multiply_reduce_fusion.1, f32[64]{0:T(128)S(1)} %get-tuple-element.59), channel_id=1, replica_groups=mesh['gx'=4,'gy'=4,'col'=2] {'gx','gy'}, use_global_device_ids=true, to_apply=%region_5.6 | all-reduce | flops 128 | bytes 1024 | tf_op jit(solution)/shard_map/psum | solution.py:89
  153.8 0.9 fusion.18
  (76 shorter events, 9.6 us)
Async XLA Ops:
  0.0 27.4 %copy-start = (f32[1,1,32,2,1152]{4,3,2,1,0:T(2,128)S(1)}, f32[1,1,32,2,1152]{4,3,2,1,0:T(2,128)}, u32[]{:S(2)}) copy-start(f32[1,1,32,2,1152]{4,3,2,1,0:T(2,128)} %param.10) | copy-start | bytes 884740
  2.4 2.5 %copy-start.2 = (f32[1,1,2,64,1152]{4,3,2,1,0:T(8,128)S(1)}, f32[1,1,2,64,1152]{4,3,2,1,0:T(8,128)}, u32[]{:S(2)}) copy-start(f32[1,1,2,64,1152]{4,3,2,1,0:T(8,128)} %param.6) | copy-start | bytes 1769476
  4.8 4.1 %copy-start.1 = (bf16[1,1,2,2,384,384]{5,4,3,2,1,0:T(8,128)(2,1)S(1)}, bf16[1,1,2,2,384,384]{5,4,3,2,1,0:T(8,128)(2,1)}, u32[]{:S(2)}) copy-start(bf16[1,1,2,2,384,384]{5,4,3,2,1,0:T(8,128)(2,1)} %param.8) | copy-start | bytes 3538948
  5.0 4.1 %copy-start.6 = (s32[1,1,2]{2,1,0:T(1,128)S(1)}, s32[1,1,2]{2,1,0:T(1,128)}, u32[]{:S(2)}) copy-start(s32[1,1,2]{2,1,0:T(1,128)} %param.9) | copy-start | bytes 28
  6.0 6.2 %collective-permute-start.2 = (bf16[2,64,192]{2,1,0:T(8,128)(2,1)S(1)}, bf16[2,64,192]{2,1,0:T(8,128)(2,1)S(1)}, u32[]{:S(2)}, u32[]{:S(2)}) collective-permute-start(bf16[2,64,192]{2,1,0:T(8,128)(2,1)S(1)} %bitcast.131), channel_id=1, source_target_pairs={{2,0},{4,2},{6,4},{3,1},{5,3},{7,5},{10,8},{12,10},{14,12},{11,9},... | collective-permute-start | bytes 147464 | tf_op jit(solution)/shard_map/ppermute | solution.py:15
  7.6 7.5 %collective-permute-start = (bf16[2,64,192]{2,1,0:T(8,128)(2,1)S(1)}, bf16[2,64,192]{2,1,0:T(8,128)(2,1)S(1)}, u32[]{:S(2)}, u32[]{:S(2)}) collective-permute-start(bf16[2,64,192]{2,1,0:T(8,128)(2,1)S(1)} %bitcast.132), channel_id=1, source_target_pairs={{8,0},{16,8},{24,16},{9,1},{17,9},{25,17},{10,2},{18,10},{26,18},{... | collective-permute-start | bytes 147464 | tf_op jit(solution)/shard_map/ppermute | solution.py:15
  11.2 0.9 copy-start.4
  12.1 10.2 %copy-start.5 = (f32[16,512]{1,0:T(8,128)S(1)}, f32[16,512]{1,0:T(8,128)}, u32[]{:S(2)}) copy-start(f32[16,512]{1,0:T(8,128)} %param.11) | copy-start | bytes 98308
  15.8 11.2 %collective-permute-start.3 = (f32[2,64,192]{2,1,0:T(8,128)S(1)}, f32[2,64,192]{2,1,0:T(8,128)S(1)}, u32[]{:S(2)}, u32[]{:S(2)}) collective-permute-start(f32[2,64,192]{2,1,0:T(8,128)S(1)} %get-tuple-element.44), channel_id=1, source_target_pairs={{0,2},{2,4},{4,6},{1,3},{3,5},{5,7},{8,10},{10,12},{12,14},{9,11},... | collective-permute-start | bytes 294920 | tf_op jit(solution)/shard_map/ppermute | solution.py:15
  18.1 8.9 %collective-permute-start.1 = (f32[2,64,192]{2,1,0:T(8,128)S(1)}, f32[2,64,192]{2,1,0:T(8,128)S(1)}, u32[]{:S(2)}, u32[]{:S(2)}) collective-permute-start(f32[2,64,192]{2,1,0:T(8,128)S(1)} %get-tuple-element.46), channel_id=1, source_target_pairs={{0,8},{8,16},{16,24},{1,9},{9,17},{17,25},{2,10},{10,18},{18,26},{... | collective-permute-start | bytes 294920 | tf_op jit(solution)/shard_map/ppermute | solution.py:15
  82.7 2.5 %copy-start.3 = (f32[1,1,2,64,1152]{4,3,2,1,0:T(8,128)S(1)}, f32[1,1,2,64,1152]{4,3,2,1,0:T(8,128)}, u32[]{:S(2)}) copy-start(f32[1,1,2,64,1152]{4,3,2,1,0:T(8,128)} %param.6) | copy-start | bytes 1769476
  85.6 3.1 %collective-permute-start.6 = (bf16[2,64,192]{2,1,0:T(8,128)(2,1)S(1)}, bf16[2,64,192]{2,1,0:T(8,128)(2,1)S(1)}, u32[]{:S(2)}, u32[]{:S(2)}) collective-permute-start(bf16[2,64,192]{2,1,0:T(8,128)(2,1)S(1)} %bitcast.133), channel_id=1, source_target_pairs={{2,0},{4,2},{6,4},{3,1},{5,3},{7,5},{10,8},{12,10},{14,12},{11,9},... | collective-permute-start | bytes 147464 | tf_op jit(solution)/shard_map/ppermute | solution.py:15
  87.3 6.7 %collective-permute-start.4 = (bf16[2,64,192]{2,1,0:T(8,128)(2,1)S(1)}, bf16[2,64,192]{2,1,0:T(8,128)(2,1)S(1)}, u32[]{:S(2)}, u32[]{:S(2)}) collective-permute-start(bf16[2,64,192]{2,1,0:T(8,128)(2,1)S(1)} %bitcast.134), channel_id=1, source_target_pairs={{8,0},{16,8},{24,16},{9,1},{17,9},{25,17},{10,2},{18,10},{26,18},{... | collective-permute-start | bytes 147464 | tf_op jit(solution)/shard_map/ppermute | solution.py:15
  94.7 4.0 %collective-permute-start.7 = (f32[2,64,192]{2,1,0:T(8,128)S(1)}, f32[2,64,192]{2,1,0:T(8,128)S(1)}, u32[]{:S(2)}, u32[]{:S(2)}) collective-permute-start(f32[2,64,192]{2,1,0:T(8,128)S(1)} %get-tuple-element.40), channel_id=1, source_target_pairs={{0,2},{2,4},{4,6},{1,3},{3,5},{5,7},{8,10},{10,12},{12,14},{9,11},... | collective-permute-start | bytes 294920 | tf_op jit(solution)/shard_map/ppermute | solution.py:15
  96.9 5.4 %collective-permute-start.5 = (f32[2,64,192]{2,1,0:T(8,128)S(1)}, f32[2,64,192]{2,1,0:T(8,128)S(1)}, u32[]{:S(2)}, u32[]{:S(2)}) collective-permute-start(f32[2,64,192]{2,1,0:T(8,128)S(1)} %get-tuple-element.42), channel_id=1, source_target_pairs={{0,8},{8,16},{16,24},{1,9},{9,17},{17,25},{2,10},{10,18},{18,26},{... | collective-permute-start | bytes 294920 | tf_op jit(solution)/shard_map/ppermute | solution.py:15
where the time goes:
time: 155 us
  blocking collectives  105 us (68%)
  matrix products  15.5 us (10%)
  starting transfers between devices  15.2 us (10%)
  waiting for transfers between devices  10.8 us (7%)
  local copies, waits for them, and re-layouts  3.56 us (2%)
  other arithmetic  3.24 us (2%)
  between operations  1.81 us (1%)
    psum x2, blocking collectives, per_device(): lax.psum((jnp.sum(defect * defect, axis=(0, 2)), jnp.sum(correction * cor...  61 us
    all_gather x2, blocking collectives, per_device(): gathered = lax.all_gather(projected[None], ('gx', 'gy'), axis=0, tiled=True)  39.2 us
    ppermute x8, starting transfers between devices, shifted(): return lax.ppermute(block, axis, route)  15.2 us
    ppermute x8, waiting for transfers between devices, shifted(): return lax.ppermute(block, axis, route)  10.8 us
    dot_general x6, matrix products, complex_apply(): jnp.dot(flattened, real_part, preferred_element_type=jnp.float32)  5.88 us
    dot_general x6, matrix products, complex_apply(): jnp.dot(flattened, imag_part, preferred_element_type=jnp.float32)  5.81 us
    all_gather x1, blocking collectives, per_device(): pair_rows = lax.all_gather(coarse_inverse, 'col', axis=0, tiled=True)  4.58 us
  transfers between devices with their start and end apart: 8, of which 4 were waited for; matrix products, arithmetic and copies ran while one was open for 3% of the time, Pallas kernels for 0%

commit v1 on v0

v1 whole, which is shorter than its diff:
```python
import jax
import jax.numpy as jnp
from jax import lax
from jax.sharding import PartitionSpec as P

ITERS = 2
STEP_RATIO = 0.4
GRID = ("gx", "gy")
EXACT = lax.Precision.HIGHEST


def shifted(block, axis, distance):
    devices = range(lax.axis_size(axis))
    return lax.ppermute(block, axis, [(i - distance, i) for i in devices if i - distance in devices])


def everyone(block):
    count = lax.axis_size(GRID)
    return lax.all_to_all(jnp.broadcast_to(block[None], (count,) + block.shape), GRID, 0, 0, tiled=True)


def complex_apply(traces, stacked_map):
    rows = traces.shape[-2]
    width = stacked_map.shape[-1] // 2
    flattened = traces.reshape(traces.shape[:-3] + (2 * rows, traces.shape[-1]))
    both = jnp.einsum("...rk,...km->...rm", flattened, stacked_map, preferred_element_type=jnp.float32)
    upper, lower = both[..., :rows, :], both[..., rows:, :]
    return jnp.stack(
        [upper[..., :width] - lower[..., width:], upper[..., width:] + lower[..., :width]], axis=-3
    )


def halves(solver, leading, face_width):
    rows_swapped = jnp.roll(solver, face_width, axis=1)
    head, tail = solver[:, :, :face_width], solver[:, :, face_width:]
    head_s, tail_s = rows_swapped[:, :, :face_width], rows_swapped[:, :, face_width:]
    return jnp.where(leading == 0, head, tail_s), jnp.where(leading == 0, tail, head_s)


def columns(solver):
    return jnp.concatenate([solver[0], solver[1]], axis=-1)


def per_device(sources, impedance, pair_maps, lead_side, coarse_basis, coarse_inverse):
    drive = sources[0, 0]
    sources_here = drive.shape[1]
    face_width = drive.shape[2] // 6
    basis = coarse_basis[0, 0]
    coarse_count = basis.shape[0]
    face = lambda traces, f: traces[..., f * face_width : (f + 1) * face_width]

    own_x, above_x = halves(pair_maps[0, 0, 0], lead_side[0, 0, 0], face_width)
    own_y, above_y = halves(pair_maps[0, 0, 1], lead_side[0, 0, 1], face_width)
    own_x = jnp.where(lax.axis_index("gx") < lax.axis_size("gx") - 1, own_x, jnp.zeros_like(own_x))
    own_y = jnp.where(lax.axis_index("gy") < lax.axis_size("gy") - 1, own_y, jnp.zeros_like(own_y))

    side = lax.axis_index("col")
    other_rows = lax.ppermute(
        coarse_inverse, "col", [(i, i ^ 1) for i in range(lax.axis_size("col"))]
    ) if lax.axis_size("col") == 2 else None
    if other_rows is None:
        rows = lax.all_gather(coarse_inverse, "col", axis=0, tiled=True)
    else:
        rows = jnp.where(
            side == 0,
            jnp.concatenate([coarse_inverse, other_rows]),
            jnp.concatenate([other_rows, coarse_inverse]),
        )
    row_blocks = rows.reshape(coarse_count, -1, coarse_count)

    solvers = None
    iterate = None
    for repeat in range(ITERS):
        if repeat == 0:
            outgoing = drive.astype(jnp.bfloat16)
            x_up = shifted(jnp.concatenate([face(outgoing, 1), above_x], axis=1), "gx", 1)
            y_up = shifted(jnp.concatenate([face(outgoing, 3), above_y], axis=1), "gy", 1)
            x_low, below_x = x_up[:, :sources_here], x_up[:, sources_here:]
            y_low, below_y = y_up[:, :sources_here], y_up[:, sources_here:]
            solvers = jnp.stack([columns(m) for m in (below_x, own_x, below_y, own_y)])
        else:
            rounded = iterate.astype(jnp.bfloat16).reshape(2 * sources_here, -1)
            first = jnp.dot(rounded, impedance[0, 0, 0], preferred_element_type=jnp.float32)
            second = jnp.dot(rounded, impedance[0, 0, 1], preferred_element_type=jnp.float32)
            product = jnp.stack(
                [first[:sources_here] - second[sources_here:], second[:sources_here] + first[sources_here:]]
            )
            outgoing = (product + drive).astype(jnp.bfloat16)
            x_low = shifted(face(outgoing, 1), "gx", 1)
            y_low = shifted(face(outgoing, 3), "gy", 1)
        x_high = shifted(face(outgoing, 0), "gx", -1)
        y_high = shifted(face(outgoing, 2), "gy", -1)
        pairs = jnp.stack(
            [
                jnp.concatenate([x_low, face(outgoing, 0)], axis=-1),
                jnp.concatenate([face(outgoing, 1), x_high], axis=-1),
                jnp.concatenate([y_low, face(outgoing, 2)], axis=-1),
                jnp.concatenate([face(outgoing, 3), y_high], axis=-1),
            ]
        )
        solved = complex_apply(pairs, solvers)
        updated = jnp.concatenate(
            [solved[0], solved[1], solved[2], solved[3],
             face(outgoing, 5).astype(jnp.float32), face(outgoing, 4).astype(jnp.float32)],
            axis=-1,
        )
        defect = updated if iterate is None else updated - iterate
        projected = jnp.einsum("csk,pck->ps", defect, basis, precision=EXACT)
        defect_part = jnp.sum(defect * defect, axis=(0, 2))
        gathered = everyone(jnp.concatenate([projected, jnp.broadcast_to(defect_part, (8, sources_here))]))
        defect_norm = jnp.sum(gathered[:, coarse_count], axis=0)
        coarse = jnp.einsum("nps,qnp->sq", gathered[:, :coarse_count], row_blocks, precision=EXACT)
        correction = jnp.einsum("sp,pck->csk", coarse, basis, precision=EXACT)
        correction_norm = jnp.sum(everyone(jnp.sum(correction * correction, axis=(0, 2))[None]), axis=(0, 1))
        factor = STEP_RATIO * jnp.sqrt(defect_norm / (correction_norm + 1e-06))
        iterate = updated + factor[None, :, None] * correction
    return iterate[None, None]


def solution(mesh):
    return jax.shard_map(
        per_device,
        mesh=mesh,
        in_specs=(
            P("gx", "gy", None, "col", None),
            P("gx", "gy", None, None, None),
            P("gx", "gy", None, None, None, None),
            P("gx", "gy", None),
            P("gx", "gy", None, None, None),
            P(("gx", "gy", "col"), None),
        ),
        out_specs=P("gx", "gy", None, "col", None),
        check_vma=False,
    )
```

time: 155 us -> 100 us (0.65)
  blocking collectives: 105 us -> 14.8 us
  starting transfers between devices: 15.2 us -> 31 us
  waiting for transfers between devices: 10.8 us -> 26.1 us
  matrix products: 15.5 us -> 9.89 us
  local copies, waits for them, and re-layouts: 3.56 us -> 8.51 us
  other arithmetic: 3.24 us -> 7.38 us
    psum x2 -> x0, blocking collectives: 61 us -> none  [per_device(): lax.psum((jnp.sum(defect * defect, axis=(0, 2)), jnp.sum(correction * cor...]
    all_gather x3 -> x0, blocking collectives: 43.7 us -> none  [the longest x2 39.2 us: per_device(): gathered = lax.all_gather(projected[None], ('gx', 'gy'), axis=0, tiled=True)]
    all_to_all x0 -> x3, waiting for transfers between devices: none -> 16.8 us  [everyone(): lax.all_to_all(jnp.broadcast_to(block[None], (count,) + block.shape), GRI...]
    all_to_all x0 -> x1, blocking collectives: none -> 14.8 us  [everyone(): lax.all_to_all(jnp.broadcast_to(block[None], (count,) + block.shape), GRI...]
    all_to_all x0 -> x3, starting transfers between devices: none -> 13.8 us  [everyone(): lax.all_to_all(jnp.broadcast_to(block[None], (count,) + block.shape), GRI...]
    dot_general x18 -> x10, matrix products: 15.5 us -> 9.89 us  [the longest x1 2.35 us: per_device(): jnp.dot(rounded, impedance[0, 0, 1], preferred_element_type=jnp.float32)]
    unnamed x22 -> x34, local copies, waits for them, and re-layouts: 0.27 us -> 2.74 us
    ppermute x8 -> x9, starting transfers between devices: 15.2 us -> 17.2 us  [the longest x8 15.7 us: shifted(): lax.ppermute(block, axis, [(i - distance, i) for i in devices if i - dist...]
  transfers between devices with their start and end apart: 8 -> 12, of which waited for: 4 -> 8; matrix products, arithmetic and copies ran while one was open for 3% -> 2% of each run, Pallas kernels for 0% -> 0%
where the time goes in v1:
time: 100 us; the launch traced here: 99.5 us
  starting transfers between devices  31 us (31%)
  waiting for transfers between devices  26.1 us (26%)
  blocking collectives  14.8 us (15%)
  matrix products  9.89 us (10%)
  local copies, waits for them, and re-layouts  8.51 us (9%)
  other arithmetic  7.38 us (7%)
  between operations  1.86 us (2%)
    all_to_all x3, waiting for transfers between devices, everyone(): lax.all_to_all(jnp.broadcast_to(block[None], (count,) + block.shape), GRI...  16.8 us
    ppermute x8, starting transfers between devices, shifted(): lax.ppermute(block, axis, [(i - distance, i) for i in devices if i - dist...  15.7 us
    all_to_all x1, blocking collectives, everyone(): lax.all_to_all(jnp.broadcast_to(block[None], (count,) + block.shape), GRI...  14.8 us
    all_to_all x3, starting transfers between devices, everyone(): lax.all_to_all(jnp.broadcast_to(block[None], (count,) + block.shape), GRI...  13.8 us
    ppermute x8, waiting for transfers between devices, shifted(): lax.ppermute(block, axis, [(i - distance, i) for i in devices if i - dist...  7.18 us
    unnamed x34, local copies, waits for them, and re-layouts  2.74 us
    dot_general x1, matrix products, per_device(): jnp.dot(rounded, impedance[0, 0, 1], preferred_element_type=jnp.float32)  2.35 us
    dot_general x1, matrix products, per_device(): jnp.dot(rounded, impedance[0, 0, 0], preferred_element_type=jnp.float32)  2.34 us
  transfers between devices with their start and end apart: 12, of which 8 were waited for; matrix products, arithmetic and copies ran while one was open for 2% of the time, Pallas kernels for 0%

profile of v1, /device:TPU:0, one launch (start us, length us, event | category | flops | bytes accessed | tf_op | source)
XLA Modules:
  0.0 99.5 jit_solution(9193804405761807787)
XLA Ops:
  0.0 1.4 %slice_bitcast_fusion.1 = (bf16[2,384,384]{2,1,0:T(8,128)(2,1)S(1)}, bf16[2,384,384]{2,1,0:T(8,128)(2,1)S(1)}) fusion(bf16[1,1,2,2,384,384]{5,4,3,2,1,0:T(8,128)(2,1)} %param.8), kind=kLoop, calls=%fused_computation.36 | loop fusion | bytes 2359296 | tf_op jit(solution)/shard_map/squeeze | solution.py:52
  5.9 5.0 %collective-permute-start = (bf16[2,448,192]{2,1,0:T(8,128)(2,1)S(1)}, bf16[2,448,192]{2,1,0:T(8,128)(2,1)S(1)}, u32[]{:S(2)}, u32[]{:S(2)}) collective-permute-start(bf16[2,448,192]{2,1,0:T(8,128)(2,1)S(1)} %pad_maximum_fusion.1), channel_id=1, source_target_pairs={{0,8},{8,16},{16,24},{1,9},{9,17},{17,25},{2,10},{10,18},{18,26},{... | collective-permute-start | bytes 1032200 | tf_op jit(solution)/shard_map/ppermute | solution.py:14
  11.0 1.5 %collective-permute-start.2 = (bf16[2,448,192]{2,1,0:T(8,128)(2,1)S(1)}, bf16[2,448,192]{2,1,0:T(8,128)(2,1)S(1)}, u32[]{:S(2)}, u32[]{:S(2)}) collective-permute-start(bf16[2,448,192]{2,1,0:T(8,128)(2,1)S(1)} %pad_maximum_fusion.2), channel_id=1, source_target_pairs={{0,2},{2,4},{4,6},{1,3},{3,5},{5,7},{8,10},{10,12},{12,14},{9,11},... | collective-permute-start | bytes 1032200 | tf_op jit(solution)/shard_map/ppermute | solution.py:14
  12.5 1.3 %collective-permute-start.1 = (bf16[2,64,192]{2,1,0:T(8,128)(2,1)S(1)}, bf16[2,64,192]{2,1,0:T(8,128)(2,1)S(1)}, u32[]{:S(2)}, u32[]{:S(2)}) collective-permute-start(bf16[2,64,192]{2,1,0:T(8,128)(2,1)S(1)} %get-tuple-element.49), channel_id=1, source_target_pairs={{8,0},{16,8},{24,16},{9,1},{17,9},{25,17},{10,2},{18,10},{26,18},{... | collective-permute-start | bytes 147464 | tf_op jit(solution)/shard_map/ppermute | solution.py:14
  13.8 1.3 %collective-permute-start.3 = (bf16[2,64,192]{2,1,0:T(8,128)(2,1)S(1)}, bf16[2,64,192]{2,1,0:T(8,128)(2,1)S(1)}, u32[]{:S(2)}, u32[]{:S(2)}) collective-permute-start(bf16[2,64,192]{2,1,0:T(8,128)(2,1)S(1)} %get-tuple-element.47), channel_id=1, source_target_pairs={{2,0},{4,2},{6,4},{3,1},{5,3},{7,5},{10,8},{12,10},{14,12},{11,9},... | collective-permute-start | bytes 147464 | tf_op jit(solution)/shard_map/ppermute | solution.py:14
  15.4 3.2 %collective-permute-done.1 = bf16[2,64,192]{2,1,0:T(8,128)(2,1)S(1)} collective-permute-done((bf16[2,64,192]{2,1,0:T(8,128)(2,1)S(1)}, bf16[2,64,192]{2,1,0:T(8,128)(2,1)S(1)}, u32[]{:S(2)}, u32[]{:S(2)}) %collective-permute-start.1) | collective-permute-done | bytes 49184 | tf_op jit(solution)/shard_map/ppermute | solution.py:14
  18.8 1.8 %collective-permute-done = bf16[2,448,192]{2,1,0:T(8,128)(2,1)S(1)} collective-permute-done((bf16[2,448,192]{2,1,0:T(8,128)(2,1)S(1)}, bf16[2,448,192]{2,1,0:T(8,128)(2,1)S(1)}, u32[]{:S(2)}, u32[]{:S(2)}) %collective-permute-start) | collective-permute-done | bytes 344096 | tf_op jit(solution)/shard_map/ppermute | solution.py:14
  25.2 6.8 %all-to-all-start = ((f32[16,1,2560]{2,1,0:T(1,128)}), f32[16,1,2560]{2,1,0:T(1,128)S(1)}, u32[]{:S(2)}, u32[]{:S(2)}) async-start(f32[16,1,2560]{2,1,0:T(1,128)} %reshape.61), calls=%async_computation | async-start | bytes 327680 | tf_op jit(solution)/shard_map/all_to_all | solution.py:19
  32.1 1.6 %collective-permute-start.4 = (f32[16,512]{1,0:T(8,128)S(1)}, f32[16,512]{1,0:T(8,128)S(1)}, u32[]{:S(2)}, u32[]{:S(2)}) collective-permute-start(f32[16,512]{1,0:T(8,128)S(1)} %copy-done.13), channel_id=1, source_target_pairs={{0,1},{1,0},{2,3},{3,2},{4,5},{5,4},{6,7},{7,6},{8,9},{9,8},{10,11... | collective-permute-start | bytes 98312 | tf_op jit(solution)/shard_map/ppermute | solution.py:58
  33.9 2.1 %collective-permute-done.4 = f32[16,512]{1,0:T(8,128)S(1)} collective-permute-done((f32[16,512]{1,0:T(8,128)S(1)}, f32[16,512]{1,0:T(8,128)S(1)}, u32[]{:S(2)}, u32[]{:S(2)}) %collective-permute-start.4) | collective-permute-done | bytes 32800 | tf_op jit(solution)/shard_map/ppermute | solution.py:58
  36.3 4.2 %all-to-all-done = f32[16,1,2560]{2,1,0:T(1,128)S(1)} async-done(((f32[16,1,2560]{2,1,0:T(1,128)}), f32[16,1,2560]{2,1,0:T(1,128)S(1)}, u32[]{:S(2)}, u32[]{:S(2)}) %all-to-all-start) | async-done | bytes 163872 | tf_op jit(solution)/shard_map/all_to_all | solution.py:19
  44.4 3.4 %all-to-all-start.1 = ((f32[16,1,64]{2,1,0:T(1,128)}), f32[16,1,64]{2,1,0:T(1,128)S(1)}, u32[]{:S(2)}, u32[]{:S(2)}) async-start(f32[16,1,64]{2,1,0:T(1,128)} %broadcast_in_dim.16), calls=%async_computation.1 | async-start | bytes 16384 | tf_op jit(solution)/shard_map/all_to_all | solution.py:19
  47.9 6.4 %all-to-all-done.1 = f32[16,1,64]{2,1,0:T(1,128)S(1)} async-done(((f32[16,1,64]{2,1,0:T(1,128)}), f32[16,1,64]{2,1,0:T(1,128)S(1)}, u32[]{:S(2)}, u32[]{:S(2)}) %all-to-all-start.1) | async-done | bytes 4128 | tf_op jit(solution)/shard_map/all_to_all | solution.py:19
  54.4 2.3 %fusion = f32[128,1152]{1,0:T(8,128)S(1)} fusion(bf16[128,1152]{1,0:T(8,128)(2,1)S(1)} %bitcast.109, bf16[1,1,2,1152,1152]{4,3,2,1,0:T(8,128)(2,1)} %param.7), kind=kOutput, calls=%fused_computation | convolution fusion | flops 339738624 | bytes 3538944 | tf_op jit(solution)/shard_map/dot_general | solution.py:84
  56.8 2.3 %fusion.2 = f32[128,1152]{1,0:T(8,128)S(1)} fusion(bf16[128,1152]{1,0:T(8,128)(2,1)S(1)} %bitcast.110, bf16[1,1,2,1152,1152]{4,3,2,1,0:T(8,128)(2,1)} %param.7), kind=kOutput, calls=%fused_computation.2 | convolution fusion | flops 339738624 | bytes 3538944 | tf_op jit(solution)/shard_map/dot_general | solution.py:83
  59.4 2.5 %collective-permute-start.5 = (bf16[2,64,192]{2,1,0:T(8,128)(2,1)S(1)}, bf16[2,64,192]{2,1,0:T(8,128)(2,1)S(1)}, u32[]{:S(2)}, u32[]{:S(2)}) collective-permute-start(bf16[2,64,192]{2,1,0:T(8,128)(2,1)S(1)} %get-tuple-element.44), channel_id=1, source_target_pairs={{0,8},{8,16},{16,24},{1,9},{9,17},{17,25},{2,10},{10,18},{18,26},{... | collective-permute-start | bytes 147464 | tf_op jit(solution)/shard_map/ppermute | solution.py:14
  62.0 1.3 %collective-permute-start.6 = (bf16[2,64,192]{2,1,0:T(8,128)(2,1)S(1)}, bf16[2,64,192]{2,1,0:T(8,128)(2,1)S(1)}, u32[]{:S(2)}, u32[]{:S(2)}) collective-permute-start(bf16[2,64,192]{2,1,0:T(8,128)(2,1)S(1)} %get-tuple-element.43), channel_id=1, source_target_pairs={{8,0},{16,8},{24,16},{9,1},{17,9},{25,17},{10,2},{18,10},{26,18},{... | collective-permute-start | bytes 147464 | tf_op jit(solution)/shard_map/ppermute | solution.py:14
  63.3 1.5 %collective-permute-start.7 = (bf16[2,64,192]{2,1,0:T(8,128)(2,1)S(1)}, bf16[2,64,192]{2,1,0:T(8,128)(2,1)S(1)}, u32[]{:S(2)}, u32[]{:S(2)}) collective-permute-start(bf16[2,64,192]{2,1,0:T(8,128)(2,1)S(1)} %get-tuple-element.42), channel_id=1, source_target_pairs={{0,2},{2,4},{4,6},{1,3},{3,5},{5,7},{8,10},{10,12},{12,14},{9,11},... | collective-permute-start | bytes 147464 | tf_op jit(solution)/shard_map/ppermute | solution.py:14
  64.7 1.3 %collective-permute-start.8 = (bf16[2,64,192]{2,1,0:T(8,128)(2,1)S(1)}, bf16[2,64,192]{2,1,0:T(8,128)(2,1)S(1)}, u32[]{:S(2)}, u32[]{:S(2)}) collective-permute-start(bf16[2,64,192]{2,1,0:T(8,128)(2,1)S(1)} %get-tuple-element.41), channel_id=1, source_target_pairs={{2,0},{4,2},{6,4},{3,1},{5,3},{7,5},{10,8},{12,10},{14,12},{11,9},... | collective-permute-start | bytes 147464 | tf_op jit(solution)/shard_map/ppermute | solution.py:14
  66.1 2.0 %collective-permute-done.6 = bf16[2,64,192]{2,1,0:T(8,128)(2,1)S(1)} collective-permute-done((bf16[2,64,192]{2,1,0:T(8,128)(2,1)S(1)}, bf16[2,64,192]{2,1,0:T(8,128)(2,1)S(1)}, u32[]{:S(2)}, u32[]{:S(2)}) %collective-permute-start.6) | collective-permute-done | bytes 49184 | tf_op jit(solution)/shard_map/ppermute | solution.py:14
  70.6 14.8 %all_to_all.20 = f32[16,1,2560]{2,1,0:T(1,128)S(1)} all-to-all(f32[16,1,2560]{2,1,0:T(1,128)S(1)} %reshape.63), channel_id=1, replica_groups=mesh['gx'=4,'gy'=4,'col'=2] {'gx','gy'}, dimensions={0} | all-to-all | bytes 327680 | tf_op jit(solution)/shard_map/all_to_all | solution.py:19
  85.4 1.0 %reduce.5 = f32[16,2560]{1,0:T(8,128)S(1)} reduce(f32[16,1,2560]{2,1,0:T(1,128)S(1)} %all_to_all.20, f32[]{:T(128)} %broadcast.43), dimensions={1}, to_apply=%all_to_all.14.reduce_sub_computation | reduce | bytes 327684 | tf_op jit(solution)/shard_map/all_to_all | solution.py:19
  88.8 3.5 %all-to-all-start.3 = ((f32[16,1,64]{2,1,0:T(1,128)}), f32[16,1,64]{2,1,0:T(1,128)S(1)}, u32[]{:S(2)}, u32[]{:S(2)}) async-start(f32[16,1,64]{2,1,0:T(1,128)} %broadcast_in_dim.38), calls=%async_computation.3 | async-start | bytes 16384 | tf_op jit(solution)/shard_map/all_to_all | solution.py:19
  92.3 6.3 %all-to-all-done.3 = f32[16,1,64]{2,1,0:T(1,128)S(1)} async-done(((f32[16,1,64]{2,1,0:T(1,128)}), f32[16,1,64]{2,1,0:T(1,128)S(1)}, u32[]{:S(2)}, u32[]{:S(2)}) %all-to-all-start.3) | async-done | bytes 4128 | tf_op jit(solution)/shard_map/all_to_all | solution.py:19
  (110 shorter events, 18.9 us)
Async XLA Ops:
  0.0 23.7 %copy-start = (f32[1,1,32,2,1152]{4,3,2,1,0:T(2,128)S(1)}, f32[1,1,32,2,1152]{4,3,2,1,0:T(2,128)}, u32[]{:S(2)}) copy-start(f32[1,1,32,2,1152]{4,3,2,1,0:T(2,128)} %param.10) | copy-start | bytes 884740
  1.4 2.7 %copy-start.1 = (f32[1,1,2,64,1152]{4,3,2,1,0:T(8,128)S(1)}, f32[1,1,2,64,1152]{4,3,2,1,0:T(8,128)}, u32[]{:S(2)}) copy-start(f32[1,1,2,64,1152]{4,3,2,1,0:T(8,128)} %param.6) | copy-start | bytes 1769476
  2.3 2.6 %copy-start.2 = (bf16[2,192,384]{2,1,0:T(8,128)(2,1)S(1)}, bf16[2,192,384]{2,1,0:T(8,128)(2,1)}, u32[]{:S(2)}) copy-start(bf16[2,192,384]{2,1,0:T(8,128)(2,1)} %get-tuple-element.22) | copy-start | bytes 884740
  5.9 14.7 %collective-permute-start = (bf16[2,448,192]{2,1,0:T(8,128)(2,1)S(1)}, bf16[2,448,192]{2,1,0:T(8,128)(2,1)S(1)}, u32[]{:S(2)}, u32[]{:S(2)}) collective-permute-start(bf16[2,448,192]{2,1,0:T(8,128)(2,1)S(1)} %pad_maximum_fusion.1), channel_id=1, source_target_pairs={{0,8},{8,16},{16,24},{1,9},{9,17},{17,25},{2,10},{10,18},{18,26},{... | collective-permute-start | bytes 1032200 | tf_op jit(solution)/shard_map/ppermute | solution.py:14
  11.0 9.7 %collective-permute-start.2 = (bf16[2,448,192]{2,1,0:T(8,128)(2,1)S(1)}, bf16[2,448,192]{2,1,0:T(8,128)(2,1)S(1)}, u32[]{:S(2)}, u32[]{:S(2)}) collective-permute-start(bf16[2,448,192]{2,1,0:T(8,128)(2,1)S(1)} %pad_maximum_fusion.2), channel_id=1, source_target_pairs={{0,2},{2,4},{4,6},{1,3},{3,5},{5,7},{8,10},{10,12},{12,14},{9,11},... | collective-permute-start | bytes 1032200 | tf_op jit(solution)/shard_map/ppermute | solution.py:14
  12.5 6.2 %collective-permute-start.1 = (bf16[2,64,192]{2,1,0:T(8,128)(2,1)S(1)}, bf16[2,64,192]{2,1,0:T(8,128)(2,1)S(1)}, u32[]{:S(2)}, u32[]{:S(2)}) collective-permute-start(bf16[2,64,192]{2,1,0:T(8,128)(2,1)S(1)} %get-tuple-element.49), channel_id=1, source_target_pairs={{8,0},{16,8},{24,16},{9,1},{17,9},{25,17},{10,2},{18,10},{26,18},{... | collective-permute-start | bytes 147464 | tf_op jit(solution)/shard_map/ppermute | solution.py:14
  13.8 5.0 %collective-permute-start.3 = (bf16[2,64,192]{2,1,0:T(8,128)(2,1)S(1)}, bf16[2,64,192]{2,1,0:T(8,128)(2,1)S(1)}, u32[]{:S(2)}, u32[]{:S(2)}) collective-permute-start(bf16[2,64,192]{2,1,0:T(8,128)(2,1)S(1)} %get-tuple-element.47), channel_id=1, source_target_pairs={{2,0},{4,2},{6,4},{3,1},{5,3},{7,5},{10,8},{12,10},{14,12},{11,9},... | collective-permute-start | bytes 147464 | tf_op jit(solution)/shard_map/ppermute | solution.py:14
  15.3 5.9 %copy-start.5 = (bf16[1,384,384]{2,1,0:T(8,128)(2,1)}, bf16[1,384,384]{2,1,0:T(8,128)(2,1)S(1)}, u32[]{:S(2)}) copy-start(bf16[1,384,384]{2,1,0:T(8,128)(2,1)S(1)} %maximum_bitcast_fusion.1) | copy-start | bytes 884740
  15.4 5.8 %copy-start.7 = (bf16[1,384,384]{2,1,0:T(8,128)(2,1)}, bf16[1,384,384]{2,1,0:T(8,128)(2,1)S(1)}, u32[]{:S(2)}) copy-start(bf16[1,384,384]{2,1,0:T(8,128)(2,1)S(1)} %maximum_bitcast_fusion.3) | copy-start | bytes 884740
  21.0 1.3 %copy-start.9 = (bf16[1,384,384]{2,1,0:T(8,128)(2,1)}, bf16[1,384,384]{2,1,0:T(8,128)(2,1)S(1)}, u32[]{:S(2)}) copy-start(bf16[1,384,384]{2,1,0:T(8,128)(2,1)S(1)} %maximum_bitcast_fusion) | copy-start | bytes 884740
  22.4 1.0 copy-start.4
  23.7 8.4 %copy-start.13 = (f32[16,512]{1,0:T(8,128)S(1)}, f32[16,512]{1,0:T(8,128)}, u32[]{:S(2)}) copy-start(f32[16,512]{1,0:T(8,128)} %param.11) | copy-start | bytes 98308
  25.2 15.3 %all-to-all-start = ((f32[16,1,2560]{2,1,0:T(1,128)}), f32[16,1,2560]{2,1,0:T(1,128)S(1)}, u32[]{:S(2)}, u32[]{:S(2)}) async-start(f32[16,1,2560]{2,1,0:T(1,128)} %reshape.61), calls=%async_computation | async-start | bytes 327680 | tf_op jit(solution)/shard_map/all_to_all | solution.py:19
  32.1 4.0 %collective-permute-start.4 = (f32[16,512]{1,0:T(8,128)S(1)}, f32[16,512]{1,0:T(8,128)S(1)}, u32[]{:S(2)}, u32[]{:S(2)}) collective-permute-start(f32[16,512]{1,0:T(8,128)S(1)} %copy-done.13), channel_id=1, source_target_pairs={{0,1},{1,0},{2,3},{3,2},{4,5},{5,4},{6,7},{7,6},{8,9},{9,8},{10,11... | collective-permute-start | bytes 98312 | tf_op jit(solution)/shard_map/ppermute | solution.py:58
  44.4 9.8 %all-to-all-start.1 = ((f32[16,1,64]{2,1,0:T(1,128)}), f32[16,1,64]{2,1,0:T(1,128)S(1)}, u32[]{:S(2)}, u32[]{:S(2)}) async-start(f32[16,1,64]{2,1,0:T(1,128)} %broadcast_in_dim.16), calls=%async_computation.1 | async-start | bytes 16384 | tf_op jit(solution)/shard_map/all_to_all | solution.py:19
  59.2 9.4 %copy-start.6 = (bf16[1,384,384]{2,1,0:T(8,128)(2,1)S(1)}, bf16[1,384,384]{2,1,0:T(8,128)(2,1)}, u32[]{:S(2)}) copy-start(bf16[1,384,384]{2,1,0:T(8,128)(2,1)} %copy-done.5) | copy-start | bytes 884740
  59.3 9.4 %copy-start.8 = (bf16[1,384,384]{2,1,0:T(8,128)(2,1)S(1)}, bf16[1,384,384]{2,1,0:T(8,128)(2,1)}, u32[]{:S(2)}) copy-start(bf16[1,384,384]{2,1,0:T(8,128)(2,1)} %copy-done.7) | copy-start | bytes 884740
  59.3 9.4 %copy-start.10 = (bf16[1,384,384]{2,1,0:T(8,128)(2,1)S(1)}, bf16[1,384,384]{2,1,0:T(8,128)(2,1)}, u32[]{:S(2)}) copy-start(bf16[1,384,384]{2,1,0:T(8,128)(2,1)} %copy-done.9) | copy-start | bytes 884740
  59.3 9.4 %copy-start.12 = (bf16[1,384,384]{2,1,0:T(8,128)(2,1)S(1)}, bf16[1,384,384]{2,1,0:T(8,128)(2,1)}, u32[]{:S(2)}) copy-start(bf16[1,384,384]{2,1,0:T(8,128)(2,1)} %copy-done.11) | copy-start | bytes 884740
  59.4 6.6 %collective-permute-start.5 = (bf16[2,64,192]{2,1,0:T(8,128)(2,1)S(1)}, bf16[2,64,192]{2,1,0:T(8,128)(2,1)S(1)}, u32[]{:S(2)}, u32[]{:S(2)}) collective-permute-start(bf16[2,64,192]{2,1,0:T(8,128)(2,1)S(1)} %get-tuple-element.44), channel_id=1, source_target_pairs={{0,8},{8,16},{16,24},{1,9},{9,17},{17,25},{2,10},{10,18},{18,26},{... | collective-permute-start | bytes 147464 | tf_op jit(solution)/shard_map/ppermute | solution.py:14
  62.0 6.2 %collective-permute-start.6 = (bf16[2,64,192]{2,1,0:T(8,128)(2,1)S(1)}, bf16[2,64,192]{2,1,0:T(8,128)(2,1)S(1)}, u32[]{:S(2)}, u32[]{:S(2)}) collective-permute-start(bf16[2,64,192]{2,1,0:T(8,128)(2,1)S(1)} %get-tuple-element.43), channel_id=1, source_target_pairs={{8,0},{16,8},{24,16},{9,1},{17,9},{25,17},{10,2},{18,10},{26,18},{... | collective-permute-start | bytes 147464 | tf_op jit(solution)/shard_map/ppermute | solution.py:14
  63.3 5.0 %collective-permute-start.7 = (bf16[2,64,192]{2,1,0:T(8,128)(2,1)S(1)}, bf16[2,64,192]{2,1,0:T(8,128)(2,1)S(1)}, u32[]{:S(2)}, u32[]{:S(2)}) collective-permute-start(bf16[2,64,192]{2,1,0:T(8,128)(2,1)S(1)} %get-tuple-element.42), channel_id=1, source_target_pairs={{0,2},{2,4},{4,6},{1,3},{3,5},{5,7},{8,10},{10,12},{12,14},{9,11},... | collective-permute-start | bytes 147464 | tf_op jit(solution)/shard_map/ppermute | solution.py:14
  64.7 3.8 %collective-permute-start.8 = (bf16[2,64,192]{2,1,0:T(8,128)(2,1)S(1)}, bf16[2,64,192]{2,1,0:T(8,128)(2,1)S(1)}, u32[]{:S(2)}, u32[]{:S(2)}) collective-permute-start(bf16[2,64,192]{2,1,0:T(8,128)(2,1)S(1)} %get-tuple-element.41), channel_id=1, source_target_pairs={{2,0},{4,2},{6,4},{3,1},{5,3},{7,5},{10,8},{12,10},{14,12},{11,9},... | collective-permute-start | bytes 147464 | tf_op jit(solution)/shard_map/ppermute | solution.py:14
  88.8 9.8 %all-to-all-start.3 = ((f32[16,1,64]{2,1,0:T(1,128)}), f32[16,1,64]{2,1,0:T(1,128)S(1)}, u32[]{:S(2)}, u32[]{:S(2)}) async-start(f32[16,1,64]{2,1,0:T(1,128)} %broadcast_in_dim.38), calls=%async_computation.3 | async-start | bytes 16384 | tf_op jit(solution)/shard_map/all_to_all | solution.py:19
  (3 other events, 2.5 us)

commit v2 on v1

v2 whole, which is shorter than its diff:
```python
import jax
import jax.numpy as jnp
from jax import lax
from jax.sharding import PartitionSpec as P

STEP_RATIO = 0.4
GRID = ("gx", "gy")
EXACT = lax.Precision.HIGHEST


def shifted(block, axis, distance):
    count = lax.axis_size(axis)
    return lax.ppermute(block, axis, [(i, (i + distance) % count) for i in range(count)])


def swap(upward, downward, axis, parity):
    count = lax.axis_size(axis)
    lows = range(parity, count, 2)
    route = [(i, (i + 1) % count) for i in lows] + [((i + 1) % count, i) for i in lows]
    mine = jnp.where(lax.axis_index(axis) % 2 == parity, upward, downward)
    return lax.ppermute(mine, axis, route)


def exchange(upward, downward, axis):
    if lax.axis_size(axis) % 2:
        return shifted(upward, axis, 1), shifted(downward, axis, -1)
    first, second = swap(upward, downward, axis, 0), swap(upward, downward, axis, 1)
    even = lax.axis_index(axis) % 2 == 0
    return jnp.where(even, second, first), jnp.where(even, first, second)


def everyone(block):
    count = lax.axis_size(GRID)
    return lax.all_to_all(jnp.broadcast_to(block[None], (count,) + block.shape), GRID, 0, 0, tiled=True)


def both_halves(rows):
    if lax.axis_size("col") != 2:
        return lax.all_gather(rows, "col", axis=0, tiled=True)
    other = lax.ppermute(rows, "col", [(0, 1), (1, 0)])
    mine_first = lax.axis_index("col") == 0
    return jnp.concatenate([jnp.where(mine_first, rows, other), jnp.where(mine_first, other, rows)])


def complex_apply(traces, stacked_map):
    rows = traces.shape[-2]
    width = stacked_map.shape[-1] // 2
    flattened = traces.reshape(traces.shape[:-3] + (2 * rows, traces.shape[-1]))
    both = jnp.einsum("...rk,...km->...rm", flattened, stacked_map, preferred_element_type=jnp.float32)
    upper, lower = both[..., :rows, :], both[..., rows:, :]
    return jnp.stack(
        [upper[..., :width] - lower[..., width:], upper[..., width:] + lower[..., :width]], axis=-3
    )


def halves(solver, leading, face_width):
    rows_swapped = jnp.roll(solver, face_width, axis=1)
    head, tail = solver[:, :, :face_width], solver[:, :, face_width:]
    head_s, tail_s = rows_swapped[:, :, :face_width], rows_swapped[:, :, face_width:]
    return jnp.where(leading == 0, head, tail_s), jnp.where(leading == 0, tail, head_s)


def columns(solver):
    return jnp.concatenate([solver[0], solver[1]], axis=-1)


def per_device(sources, impedance, pair_maps, lead_side, coarse_basis, coarse_inverse):
    drive = sources[0, 0]
    count = drive.shape[1]
    face_width = drive.shape[2] // 6
    basis = coarse_basis[0, 0]
    coarse_count = basis.shape[0]
    face = lambda traces, f: traces[..., f * face_width : (f + 1) * face_width]

    own_x, above_x = halves(pair_maps[0, 0, 0], lead_side[0, 0, 0], face_width)
    own_y, above_y = halves(pair_maps[0, 0, 1], lead_side[0, 0, 1], face_width)
    inner_x = lax.axis_index("gx") < lax.axis_size("gx") - 1
    inner_y = lax.axis_index("gy") < lax.axis_size("gy") - 1
    own_x, above_x = (jnp.where(inner_x, m, jnp.zeros_like(m)) for m in (own_x, above_x))
    own_y, above_y = (jnp.where(inner_y, m, jnp.zeros_like(m)) for m in (own_y, above_y))

    def joined(parts, outgoing):
        return jnp.concatenate(
            parts + [face(outgoing, 5).astype(jnp.float32), face(outgoing, 4).astype(jnp.float32)], axis=-1
        )

    def project(defect):
        return jnp.einsum("csk,pck->ps", defect, basis, precision=EXACT)

    outgoing = drive.astype(jnp.bfloat16)
    high_y = shifted(face(outgoing, 2), "gy", -1)
    high_x = shifted(face(outgoing, 0), "gx", -1)
    pairs = jnp.stack(
        [jnp.concatenate([face(outgoing, 3), high_y], axis=-1), jnp.concatenate([face(outgoing, 1), high_x], axis=-1)]
    )
    whole = jnp.stack(
        [columns(jnp.concatenate([own_y, above_y], axis=-1)), columns(jnp.concatenate([own_x, above_x], axis=-1))]
    )
    solved = complex_apply(pairs, whole)
    face_two = shifted(solved[0, :, :, face_width:], "gy", 1)
    face_zero = shifted(solved[1, :, :, face_width:], "gx", 1)
    updated = joined([face_zero, solved[1, :, :, :face_width], face_two, solved[0, :, :, :face_width]], outgoing)
    projected = project(updated)
    half = coarse_count // 2
    payload = jnp.concatenate([projected[:half], projected[half:]], axis=1)
    payload, above_y, above_x, part_rows, state, rounded_basis = lax.optimization_barrier(
        (payload, above_y, above_x, coarse_inverse, updated, basis.transpose(1, 0, 2).astype(jnp.bfloat16))
    )
    gathered = everyone(payload)
    below_y, below_x = (
        shifted(jnp.concatenate([m[:, :face_width], m[:, face_width:]], axis=-1), axis, 1)
        for m, axis in ((above_y, "gy"), (above_x, "gx"))
    )
    rows = both_halves(part_rows)
    row_blocks = rows.reshape(coarse_count, -1, coarse_count)

    rounded = jnp.concatenate([state.astype(jnp.bfloat16), rounded_basis], axis=1)
    total = count + coarse_count
    rounded = rounded.reshape(2 * total, -1)
    first = jnp.dot(rounded, impedance[0, 0, 0], preferred_element_type=jnp.float32)
    second = jnp.dot(rounded, impedance[0, 0, 1], preferred_element_type=jnp.float32)
    product = jnp.stack([first[:total] - second[total:], second[:total] + first[total:]])
    defect_part = jnp.sum(updated * updated, axis=(0, 2))

    gathered = jnp.concatenate([gathered[:, :, :count], gathered[:, :, count:]], axis=1)
    coarse = jnp.einsum("nps,qnp->sq", gathered, row_blocks, precision=EXACT)
    correction = jnp.einsum("sp,pck->csk", coarse, basis, precision=EXACT)
    correction_part = jnp.sum(correction * correction, axis=(0, 2))
    response = jnp.einsum("sp,cpk->csk", coarse, product[:, count:], precision=lax.Precision.HIGH)
    outgoing = jnp.concatenate([product[:, :count] + drive, response], axis=1).astype(jnp.bfloat16)
    low_y, high_y = exchange(face(outgoing, 3), face(outgoing, 2), "gy")
    low_x, high_x = exchange(face(outgoing, 1), face(outgoing, 0), "gx")
    below_x, below_y = (
        jnp.concatenate([m[:, :, :face_width], m[:, :, face_width:]], axis=1) for m in (below_x, below_y)
    )
    solvers = jnp.stack([columns(m) for m in (below_x, own_x, below_y, own_y)])
    pairs = jnp.stack(
        [
            jnp.concatenate([low_x, face(outgoing, 0)], axis=-1),
            jnp.concatenate([face(outgoing, 1), high_x], axis=-1),
            jnp.concatenate([low_y, face(outgoing, 2)], axis=-1),
            jnp.concatenate([face(outgoing, 3), high_y], axis=-1),
        ]
    )
    solved = complex_apply(pairs, solvers)
    both = joined([solved[0], solved[1], solved[2], solved[3]], outgoing)
    defects = both - jnp.concatenate([updated, correction], axis=1)
    sums = jnp.concatenate([defect_part, correction_part])
    gathered = everyone(jnp.concatenate([project(defects), jnp.broadcast_to(sums, (8, 2 * count))]))
    totals = jnp.sum(gathered[:, coarse_count], axis=0)
    factor = STEP_RATIO * jnp.sqrt(totals[:count] / (totals[count:] + 1e-06))
    gathered = gathered[:, :coarse_count]
    gathered = gathered[:, :, :count] + factor * gathered[:, :, count:]
    defect = defects[:, :count] + factor[None, :, None] * defects[:, count:]
    updated = both[:, :count] + factor[None, :, None] * both[:, count:]
    coarse = jnp.einsum("nps,qnp->sq", gathered, row_blocks, precision=EXACT)
    correction = jnp.einsum("sp,pck->csk", coarse, basis, precision=EXACT)
    sums = jnp.concatenate([jnp.sum(defect * defect, axis=(0, 2)), jnp.sum(correction * correction, axis=(0, 2))])
    totals = jnp.sum(everyone(sums[None]), axis=(0, 1))
    factor = STEP_RATIO * jnp.sqrt(totals[:count] / (totals[count:] + 1e-06))
    iterate = updated + factor[None, :, None] * correction
    return iterate[None, None]


def solution(mesh):
    return jax.shard_map(
        per_device,
        mesh=mesh,
        in_specs=(
            P("gx", "gy", None, "col", None),
            P("gx", "gy", None, None, None),
            P("gx", "gy", None, None, None, None),
            P("gx", "gy", None),
            P("gx", "gy", None, None, None),
            P(("gx", "gy", "col"), None),
        ),
        out_specs=P("gx", "gy", None, "col", None),
        check_vma=False,
    )
```

time: 100 us -> 89.8 us (0.90)
  starting transfers between devices: 31 us -> 14.7 us
  waiting for transfers between devices: 26.1 us -> 13 us
  blocking collectives: 14.8 us -> 23.3 us
  other arithmetic: 7.38 us -> 14.6 us
  matrix products: 9.89 us -> 12.9 us
    all_to_all x3 -> x1, waiting for transfers between devices: 16.8 us -> 3.53 us  [everyone(): lax.all_to_all(jnp.broadcast_to(block[None], (count,) + block.shape), GRI...]
    all_to_all x3 -> x1, starting transfers between devices: 13.8 us -> 3.51 us  [everyone(): lax.all_to_all(jnp.broadcast_to(block[None], (count,) + block.shape), GRI...]
    all_to_all x1 -> x2, blocking collectives: 14.8 us -> 23.3 us  [everyone(): lax.all_to_all(jnp.broadcast_to(block[None], (count,) + block.shape), GRI...]
    ppermute x9 -> x11, starting transfers between devices: 17.2 us -> 11.2 us  [the longest x6 7.98 us: shifted(): lax.ppermute(block, axis, [(i, (i + distance) % count) for i in range(cou...]
    concatenate x12 -> x14, other arithmetic: 0.89 us -> 4.28 us  [the longest x2 1.71 us: per_device(): jnp.concatenate([m[:, :face_width], m[:, face_width:]], axis=-1)]
    slice x6 -> x7, local copies, waits for them, and re-layouts: 0.06 us -> 2.43 us  [the longest x2 2.28 us: per_device(): m[:, :, :face_width]]
    all_to_all x2 -> x0, other arithmetic: 2.03 us -> none  [everyone(): lax.all_to_all(jnp.broadcast_to(block[None], (count,) + block.shape), GRI...]
    squeeze x2 -> x6, other arithmetic: 0.08 us -> 1.56 us  [the longest x1 0.86 us: per_device(): both = joined([solved[0], solved[1], solved[2], solved[3]], outgoing)]
  transfers between devices with their start and end apart: 12 -> 12, of which waited for: 8 -> 5; matrix products, arithmetic and copies ran while one was open for 2% -> 16% of each run, Pallas kernels for 0% -> 0%
where the time goes in v2:
time: 89.8 us; the launch traced here: 89.1 us
  blocking collectives  23.3 us (26%)
  starting transfers between devices  14.7 us (16%)
  other arithmetic  14.6 us (16%)
  waiting for transfers between devices  13 us (14%)
  matrix products  12.9 us (14%)
  local copies, waits for them, and re-layouts  8.87 us (10%)
  between operations  1.78 us (2%)
    all_to_all x2, blocking collectives, everyone(): lax.all_to_all(jnp.broadcast_to(block[None], (count,) + block.shape), GRI...  23.3 us
    ppermute x6, starting transfers between devices, shifted(): lax.ppermute(block, axis, [(i, (i + distance) % count) for i in range(cou...  7.98 us
    ppermute x6, waiting for transfers between devices, shifted(): lax.ppermute(block, axis, [(i, (i + distance) % count) for i in range(cou...  6.7 us
    all_to_all x1, waiting for transfers between devices, everyone(): lax.all_to_all(jnp.broadcast_to(block[None], (count,) + block.shape), GRI...  3.53 us
    all_to_all x1, starting transfers between devices, everyone(): lax.all_to_all(jnp.broadcast_to(block[None], (count,) + block.shape), GRI...  3.51 us
    dot_general x1, matrix products, per_device(): jnp.dot(rounded, impedance[0, 0, 0], preferred_element_type=jnp.float32)  3.49 us
    unnamed x27, local copies, waits for them, and re-layouts  3.02 us
    ppermute x4, waiting for transfers between devices, swap(): return lax.ppermute(mine, axis, route)  2.72 us
  transfers between devices with their start and end apart: 12, of which 5 were waited for; matrix products, arithmetic and copies ran while one was open for 16% of the time, Pallas kernels for 0%

profile of v2, /device:TPU:0, one launch (start us, length us, event | category | flops | bytes accessed | tf_op | source)
XLA Modules:
  0.0 89.1 jit_solution(15280678305469691624)
XLA Ops:
  0.0 1.2 %bitcast_convert_fusion = bf16[2,64,1152]{2,1,0:T(8,128)(2,1)S(1)} fusion(f32[1,1,2,64,1152]{4,3,2,1,0:T(8,128)} %param.6), kind=kLoop, calls=%fused_computation.70 | loop fusion | flops 147456 | bytes 884736 | tf_op jit(solution)/shard_map/convert_element_type | solution.py:90
  2.0 2.4 %collective-permute-start = (bf16[2,64,192]{2,1,0:T(8,128)(2,1)}, bf16[2,64,192]{2,1,0:T(8,128)(2,1)}, u32[]{:S(2)}, u32[]{:S(2)}) collective-permute-start(bf16[2,64,192]{2,1,0:T(8,128)(2,1)} %get-tuple-element.76), channel_id=1, source_target_pairs={{0,6},{2,0},{4,2},{6,4},{1,7},{3,1},{5,3},{7,5},{8,14},{10,8},{12,... | collective-permute-start | bytes 147464 | tf_op jit(solution)/shard_map/ppermute | solution.py:13
  4.5 3.6 %collective-permute-start.1 = (bf16[2,64,192]{2,1,0:T(8,128)(2,1)}, bf16[2,64,192]{2,1,0:T(8,128)(2,1)}, u32[]{:S(2)}, u32[]{:S(2)}) collective-permute-start(bf16[2,64,192]{2,1,0:T(8,128)(2,1)} %get-tuple-element.74), channel_id=1, source_target_pairs={{0,24},{8,0},{16,8},{24,16},{1,25},{9,1},{17,9},{25,17},{2,26},{10... | collective-permute-start | bytes 147464 | tf_op jit(solution)/shard_map/ppermute | solution.py:13
  10.8 1.1 %fusion.41 = (bf16[2,384,192]{2,1,0:T(8,128)(2,1)S(1)}, bf16[2,384,192]{2,1,0:T(8,128)(2,1)S(1)}, bf16[2,384,192]{2,1,0:T(8,128)(2,1)S(1)}, bf16[2,384,192]{2,1,0:T(8,128)(2,1)S(1)}) fusion(bf16[2,192,384]{2,1,0:T(8,128)(2,1)S(1)} %get-tuple-element.48, bf16[2,192,384]{2,1,0:T(8,128)(2,1)S(1)} %get-tuple-element.49, ...), kind=kLoop, calls=%fused_computation.93 | loop fusion | flops 3538944 | bytes 3538948 | tf_op jit(solution)/shard_map/jit(_where)/select_n | solution.py:79
  13.4 0.9 %pad_maximum_fusion.18 = bf16[2,64,384]{2,1,0:T(8,128)(2,1)S(1)} fusion(bf16[2,64,192]{2,1,0:T(8,128)(2,1)} %collective-permute-done, bf16[2,64,192]{2,1,0:T(8,128)(2,1)S(1)} %copy-done.10), kind=kLoop, calls=%fused_computation.198 | loop fusion | flops 196608 | bytes 196608 | tf_op jit(solution)/shard_map/concatenate | solution.py:94
  16.8 5.8 %collective-permute-done.2 = f32[2,64,192]{2,1,0:T(8,128)S(1)} collective-permute-done((f32[2,64,192]{2,1,0:T(8,128)S(1)}, f32[2,64,192]{2,1,0:T(8,128)S(1)}, u32[]{:S(2)}, u32[]{:S(2)}) %collective-permute-start.2) | collective-permute-done | bytes 98336 | tf_op jit(solution)/shard_map/ppermute | solution.py:13
  23.7 2.5 %fusion = f32[192,1152]{1,0:T(8,128)S(1)} fusion(bf16[192,1152]{1,0:T(8,128)(2,1)S(1)} %bitcast.145, bf16[1,1,2,1152,1152]{4,3,2,1,0:T(8,128)(2,1)} %param.7), kind=kOutput, calls=%fused_computation | convolution fusion | flops 509607936 | bytes 3981312 | tf_op jit(solution)/shard_map/dot_general | solution.py:121
  26.2 3.5 %fusion.2 = f32[192,1152]{1,0:T(8,128)} fusion(bf16[192,1152]{1,0:T(8,128)(2,1)S(1)} %bitcast.146, bf16[1,1,2,1152,1152]{4,3,2,1,0:T(8,128)(2,1)} %param.7), kind=kOutput, calls=%fused_computation.2 | convolution fusion | flops 509607936 | bytes 3981312 | tf_op jit(solution)/shard_map/dot_general | solution.py:120
  29.9 1.6 %collective-permute-start.4 = (f32[16,512]{1,0:T(8,128)S(1)}, f32[16,512]{1,0:T(8,128)S(1)}, u32[]{:S(2)}, u32[]{:S(2)}) collective-permute-start(f32[16,512]{1,0:T(8,128)S(1)} %copy-done.11), channel_id=1, source_target_pairs={{0,1},{1,0},{2,3},{3,2},{4,5},{5,4},{6,7},{7,6},{8,9},{9,8},{10,11... | collective-permute-start | bytes 98312 | tf_op jit(solution)/shard_map/ppermute | solution.py:40
  32.1 3.5 %all-to-all-start = ((f32[16,16,128]{2,1,0:T(8,128)}), f32[16,16,128]{2,1,0:T(8,128)S(1)}, u32[]{:S(2)}, u32[]{:S(2)}) async-start(f32[16,16,128]{2,1,0:T(8,128)} %broadcast_in_dim.10), calls=%async_computation | async-start | bytes 262144 | tf_op jit(solution)/shard_map/all_to_all | solution.py:34
  36.5 1.8 %collective-permute-start.9 = (bf16[2,192,384]{2,1,0:T(8,128)(2,1)}, bf16[2,192,384]{2,1,0:T(8,128)(2,1)}, u32[]{:S(2)}, u32[]{:S(2)}) collective-permute-start(bf16[2,192,384]{2,1,0:T(8,128)(2,1)} %pad_maximum_fusion.7), channel_id=1, source_target_pairs={{0,8},{8,16},{16,24},{24,0},{1,9},{9,17},{17,25},{25,1},{2,10},{10... | collective-permute-start | bytes 884744 | tf_op jit(solution)/shard_map/ppermute | solution.py:13
  39.3 1.0 %copy-done.1 = f32[1,1,2,64,1152]{4,3,2,1,0:T(8,128)S(1)} copy-done((f32[1,1,2,64,1152]{4,3,2,1,0:T(8,128)S(1)}, f32[1,1,2,64,1152]{4,3,2,1,0:T(8,128)}, u32[]{:S(2)}) %copy-start.1) | copy-done | bytes 589848
  40.5 3.5 %all-to-all-done = f32[16,16,128]{2,1,0:T(8,128)S(1)} async-done(((f32[16,16,128]{2,1,0:T(8,128)}), f32[16,16,128]{2,1,0:T(8,128)S(1)}, u32[]{:S(2)}, u32[]{:S(2)}) %all-to-all-start) | async-done | bytes 131104 | tf_op jit(solution)/shard_map/all_to_all | solution.py:34
  45.5 1.4 %collective-permute-start.5 = (bf16[2,128,192]{2,1,0:T(8,128)(2,1)S(1)}, bf16[2,128,192]{2,1,0:T(8,128)(2,1)S(1)}, u32[]{:S(2)}, u32[]{:S(2)}) collective-permute-start(bf16[2,128,192]{2,1,0:T(8,128)(2,1)S(1)} %get-tuple-element.17), channel_id=1, source_target_pairs={{8,16},{24,0},{16,8},{0,24},{9,17},{25,1},{17,9},{1,25},{10,18},{2... | collective-permute-start | bytes 294920 | tf_op jit(solution)/shard_map/ppermute | solution.py:21
  47.0 1.6 %multiply_reduce_fusion.1 = (f32[64]{0:T(128)S(1)}, f32[2,64,1152]{2,1,0:T(8,128)}) fusion(f32[64,32,1]{0,1,2:T(8,128)S(1)} %fusion.72, f32[1,1,32,2,1152]{4,3,2,1,0:T(2,128)S(1)} %copy-done), kind=kOutput, calls=%fused_computation.72 | convolution fusion | flops 56917952 | bytes 893184 | tf_op jit(solution)/shard_map/sp,pck->csk/dot_general | solution.py:127
  49.6 1.1 %fusion.119 = (bf16[2,192,192]{2,1,0:T(8,128)(2,1)S(1)}, bf16[2,192,192]{2,1,0:T(8,128)(2,1)S(1)}) fusion(bf16[2,192,384]{2,1,0:T(8,128)(2,1)} %collective-permute-done.9), kind=kLoop, calls=%fused_computation.221 | loop fusion | bytes 589824 | tf_op jit(solution)/shard_map/slice | solution.py:134
  51.0 1.1 %fusion.120 = (bf16[2,192,192]{2,1,0:T(8,128)(2,1)S(1)}, bf16[2,192,192]{2,1,0:T(8,128)(2,1)S(1)}) fusion(bf16[2,192,384]{2,1,0:T(8,128)(2,1)} %collective-permute-done.10), kind=kLoop, calls=%fused_computation.222 | loop fusion | bytes 589824 | tf_op jit(solution)/shard_map/slice | solution.py:134
  52.3 2.3 %collective-permute-done.5 = bf16[2,128,192]{2,1,0:T(8,128)(2,1)S(1)} collective-permute-done((bf16[2,128,192]{2,1,0:T(8,128)(2,1)S(1)}, bf16[2,128,192]{2,1,0:T(8,128)(2,1)S(1)}, u32[]{:S(2)}, u32[]{:S(2)}) %collective-permute-start.5) | collective-permute-done | bytes 98336 | tf_op jit(solution)/shard_map/ppermute | solution.py:21
  57.6 1.4 %concatenate.123 = f32[2,128,1152]{2,1,0:T(8,128)S(1)} concatenate(f32[2,128,192]{2,1,0:T(8,128)S(1)} %get-tuple-element.34, f32[2,128,192]{2,1,0:T(8,128)} %get-tuple-element.35, f32[2,128,192]{2,1,0:T(8,128)} %get-tuple-element.36, f32[2,128,192]{2,1,0:T(8,128)S(1)} %get-tuple-element.33, f32[2,128,192]{2,1,0:T(8,128)S(1)} %get-tuple-element.44, ...), dimensions={2} | concatenate | bytes 2359296 | tf_op jit(solution)/shard_map/concatenate | solution.py:83
  59.0 1.2 %maximum_subtract_fusion = f32[2,128,1152]{2,1,0:T(8,128)S(1)} fusion(f32[2,128,1152]{2,1,0:T(8,128)S(1)} %concatenate.123, f32[2,64,1152]{2,1,0:T(8,128)} %get-tuple-element.91, f32[2,64,1152]{2,1,0:T(8,128)S(1)} %concatenate.105), kind=kLoop, calls=%fused_computation.27 | loop fusion | flops 589824 | bytes 3538944 | tf_op jit(solution)/shard_map/sub | solution.py:147
  60.2 1.2 %convolution_bitcast_fusion.1 = f32[32,128]{1,0:T(8,128)S(1)} fusion(f32[2,128,1152]{2,1,0:T(8,128)S(1)} %maximum_subtract_fusion, f32[1,1,32,2,1152]{4,3,2,1,0:T(2,128)S(1)} %copy-done), kind=kOutput, calls=%fused_computation.28 | convolution fusion | flops 113246208 | bytes 1490944 | tf_op jit(solution)/shard_map/csk,pck->ps/dot_general | solution.py:88
  61.4 13.9 %all_to_all.15 = f32[16,40,128]{2,1,0:T(8,128)S(1)} all-to-all(f32[16,40,128]{2,1,0:T(8,128)S(1)} %broadcast_in_dim.12), channel_id=1, replica_groups=mesh['gx'=4,'gy'=4,'col'=2] {'gx','gy'}, dimensions={0} | all-to-all | bytes 655360 | tf_op jit(solution)/shard_map/all_to_all | solution.py:34
  78.6 9.4 %all_to_all.16 = f32[16,1,128]{2,1,0:T(1,128)S(1)} all-to-all(f32[16,1,128]{2,1,0:T(1,128)S(1)} %broadcast_in_dim.13), channel_id=1, replica_groups=mesh['gx'=4,'gy'=4,'col'=2] {'gx','gy'}, dimensions={0} | all-to-all | bytes 16384 | tf_op jit(solution)/shard_map/all_to_all | solution.py:34
  88.1 1.0 %fusion.34 = f32[1,1,2,64,1152]{4,3,2,1,0:T(8,128)} fusion(f32[2,128,1152]{2,1,0:T(8,128)S(1)} %concatenate.123, f32[64,2,1152]{2,0,1:T(8,128)S(1)} %get-tuple-element.93, f32[64]{0:T(128)S(1)} %sqrt_multiply_fusion, f32[64]{0:T(128)S(1)} %sqrt_multiply_fusion.1), kind=kLoop, calls=%fused_computation.59 | loop fusion | flops 589824 | bytes 2359808 | tf_op jit(solution)/shard_map/broadcast_in_dim | solution.py:162
  (108 shorter events, 19.1 us)
Async XLA Ops:
  0.0 8.1 %copy-start.2 = (bf16[1,1,2,2,384,384]{5,4,3,2,1,0:T(8,128)(2,1)S(1)}, bf16[1,1,2,2,384,384]{5,4,3,2,1,0:T(8,128)(2,1)}, u32[]{:S(2)}) copy-start(bf16[1,1,2,2,384,384]{5,4,3,2,1,0:T(8,128)(2,1)} %param.8) | copy-start | bytes 3538948
  2.0 11.4 %collective-permute-start = (bf16[2,64,192]{2,1,0:T(8,128)(2,1)}, bf16[2,64,192]{2,1,0:T(8,128)(2,1)}, u32[]{:S(2)}, u32[]{:S(2)}) collective-permute-start(bf16[2,64,192]{2,1,0:T(8,128)(2,1)} %get-tuple-element.76), channel_id=1, source_target_pairs={{0,6},{2,0},{4,2},{6,4},{1,7},{3,1},{5,3},{7,5},{8,14},{10,8},{12,... | collective-permute-start | bytes 147464 | tf_op jit(solution)/shard_map/ppermute | solution.py:13
  4.5 9.9 %collective-permute-start.1 = (bf16[2,64,192]{2,1,0:T(8,128)(2,1)}, bf16[2,64,192]{2,1,0:T(8,128)(2,1)}, u32[]{:S(2)}, u32[]{:S(2)}) collective-permute-start(bf16[2,64,192]{2,1,0:T(8,128)(2,1)} %get-tuple-element.74), channel_id=1, source_target_pairs={{0,24},{8,0},{16,8},{24,16},{1,25},{9,1},{17,9},{25,17},{2,26},{10... | collective-permute-start | bytes 147464 | tf_op jit(solution)/shard_map/ppermute | solution.py:13
  12.4 1.0 %copy-start = (f32[1,1,32,2,1152]{4,3,2,1,0:T(2,128)S(1)}, f32[1,1,32,2,1152]{4,3,2,1,0:T(2,128)}, u32[]{:S(2)}) copy-start(f32[1,1,32,2,1152]{4,3,2,1,0:T(2,128)} %param.10) | copy-start | bytes 884740
  12.5 0.9 %copy-start.10 = (bf16[2,64,192]{2,1,0:T(8,128)(2,1)S(1)}, bf16[2,64,192]{2,1,0:T(8,128)(2,1)}, u32[]{:S(2)}) copy-start(bf16[2,64,192]{2,1,0:T(8,128)(2,1)} %get-tuple-element.77) | copy-start | bytes 147460
  12.5 1.9 %copy-start.9 = (bf16[2,64,192]{2,1,0:T(8,128)(2,1)S(1)}, bf16[2,64,192]{2,1,0:T(8,128)(2,1)}, u32[]{:S(2)}) copy-start(bf16[2,64,192]{2,1,0:T(8,128)(2,1)} %get-tuple-element.75) | copy-start | bytes 147460
  15.7 7.0 %copy-start.6 = (f32[2,64,192]{2,1,0:T(8,128)S(1)}, f32[2,64,192]{2,1,0:T(8,128)}, u32[]{:S(2)}) copy-start(f32[2,64,192]{2,1,0:T(8,128)} %get-tuple-element.73) | copy-start | bytes 294916
  15.9 6.8 %collective-permute-start.2 = (f32[2,64,192]{2,1,0:T(8,128)S(1)}, f32[2,64,192]{2,1,0:T(8,128)S(1)}, u32[]{:S(2)}, u32[]{:S(2)}) collective-permute-start(f32[2,64,192]{2,1,0:T(8,128)S(1)} %get-tuple-element.63), channel_id=1, source_target_pairs={{0,8},{8,16},{16,24},{24,0},{1,9},{9,17},{17,25},{25,1},{2,10},{10... | collective-permute-start | bytes 294920 | tf_op jit(solution)/shard_map/ppermute | solution.py:13
  15.9 6.8 %collective-permute-start.3 = (f32[2,64,192]{2,1,0:T(8,128)S(1)}, f32[2,64,192]{2,1,0:T(8,128)S(1)}, u32[]{:S(2)}, u32[]{:S(2)}) collective-permute-start(f32[2,64,192]{2,1,0:T(8,128)S(1)} %get-tuple-element.65), channel_id=1, source_target_pairs={{0,2},{2,4},{4,6},{6,0},{1,3},{3,5},{5,7},{7,1},{8,10},{10,12},{12... | collective-permute-start | bytes 294920 | tf_op jit(solution)/shard_map/ppermute | solution.py:13
  26.2 3.6 %copy-start.11 = (f32[16,512]{1,0:T(8,128)S(1)}, f32[16,512]{1,0:T(8,128)}, u32[]{:S(2)}) copy-start(f32[16,512]{1,0:T(8,128)} %param.11) | copy-start | bytes 98308
  29.9 10.5 %collective-permute-start.4 = (f32[16,512]{1,0:T(8,128)S(1)}, f32[16,512]{1,0:T(8,128)S(1)}, u32[]{:S(2)}, u32[]{:S(2)}) collective-permute-start(f32[16,512]{1,0:T(8,128)S(1)} %copy-done.11), channel_id=1, source_target_pairs={{0,1},{1,0},{2,3},{3,2},{4,5},{5,4},{6,7},{7,6},{8,9},{9,8},{10,11... | collective-permute-start | bytes 98312 | tf_op jit(solution)/shard_map/ppermute | solution.py:40
  32.1 12.0 %all-to-all-start = ((f32[16,16,128]{2,1,0:T(8,128)}), f32[16,16,128]{2,1,0:T(8,128)S(1)}, u32[]{:S(2)}, u32[]{:S(2)}) async-start(f32[16,16,128]{2,1,0:T(8,128)} %broadcast_in_dim.10), calls=%async_computation | async-start | bytes 262144 | tf_op jit(solution)/shard_map/all_to_all | solution.py:34
  35.6 3.6 %copy-start.5 = (f32[192,1152]{1,0:T(8,128)S(1)}, f32[192,1152]{1,0:T(8,128)}, u32[]{:S(2)}) copy-start(f32[192,1152]{1,0:T(8,128)} %fusion.2) | copy-start | bytes 2654212
  36.5 13.1 %collective-permute-start.9 = (bf16[2,192,384]{2,1,0:T(8,128)(2,1)}, bf16[2,192,384]{2,1,0:T(8,128)(2,1)}, u32[]{:S(2)}, u32[]{:S(2)}) collective-permute-start(bf16[2,192,384]{2,1,0:T(8,128)(2,1)} %pad_maximum_fusion.7), channel_id=1, source_target_pairs={{0,8},{8,16},{16,24},{24,0},{1,9},{9,17},{17,25},{25,1},{2,10},{10... | collective-permute-start | bytes 884744 | tf_op jit(solution)/shard_map/ppermute | solution.py:13
  39.2 1.1 %copy-start.1 = (f32[1,1,2,64,1152]{4,3,2,1,0:T(8,128)S(1)}, f32[1,1,2,64,1152]{4,3,2,1,0:T(8,128)}, u32[]{:S(2)}) copy-start(f32[1,1,2,64,1152]{4,3,2,1,0:T(8,128)} %param.6) | copy-start | bytes 1769476
  39.2 11.7 %collective-permute-start.10 = (bf16[2,192,384]{2,1,0:T(8,128)(2,1)}, bf16[2,192,384]{2,1,0:T(8,128)(2,1)}, u32[]{:S(2)}, u32[]{:S(2)}) collective-permute-start(bf16[2,192,384]{2,1,0:T(8,128)(2,1)} %pad_maximum_fusion.8), channel_id=1, source_target_pairs={{0,2},{2,4},{4,6},{6,0},{1,3},{3,5},{5,7},{7,1},{8,10},{10,12},{12... | collective-permute-start | bytes 884744 | tf_op jit(solution)/shard_map/ppermute | solution.py:13
  45.4 6.9 %collective-permute-start.6 = (bf16[2,128,192]{2,1,0:T(8,128)(2,1)S(1)}, bf16[2,128,192]{2,1,0:T(8,128)(2,1)S(1)}, u32[]{:S(2)}, u32[]{:S(2)}) collective-permute-start(bf16[2,128,192]{2,1,0:T(8,128)(2,1)S(1)} %broadcast_select_fusion.7), channel_id=1, source_target_pairs={{0,8},{16,24},{8,0},{24,16},{1,9},{17,25},{9,1},{25,17},{2,10},{18... | collective-permute-start | bytes 294920 | tf_op jit(solution)/shard_map/ppermute | solution.py:21
  45.5 9.1 %collective-permute-start.5 = (bf16[2,128,192]{2,1,0:T(8,128)(2,1)S(1)}, bf16[2,128,192]{2,1,0:T(8,128)(2,1)S(1)}, u32[]{:S(2)}, u32[]{:S(2)}) collective-permute-start(bf16[2,128,192]{2,1,0:T(8,128)(2,1)S(1)} %get-tuple-element.17), channel_id=1, source_target_pairs={{8,16},{24,0},{16,8},{0,24},{9,17},{25,1},{17,9},{1,25},{10,18},{2... | collective-permute-start | bytes 294920 | tf_op jit(solution)/shard_map/ppermute | solution.py:21
  47.0 7.9 %collective-permute-start.8 = (bf16[2,128,192]{2,1,0:T(8,128)(2,1)S(1)}, bf16[2,128,192]{2,1,0:T(8,128)(2,1)S(1)}, u32[]{:S(2)}, u32[]{:S(2)}) collective-permute-start(bf16[2,128,192]{2,1,0:T(8,128)(2,1)S(1)} %broadcast_select_fusion.3), channel_id=1, source_target_pairs={{0,2},{4,6},{2,0},{6,4},{1,3},{5,7},{3,1},{7,5},{8,10},{12,14},{10... | collective-permute-start | bytes 294920 | tf_op jit(solution)/shard_map/ppermute | solution.py:21
  49.6 5.8 %collective-permute-start.7 = (bf16[2,128,192]{2,1,0:T(8,128)(2,1)S(1)}, bf16[2,128,192]{2,1,0:T(8,128)(2,1)S(1)}, u32[]{:S(2)}, u32[]{:S(2)}) collective-permute-start(bf16[2,128,192]{2,1,0:T(8,128)(2,1)S(1)} %get-tuple-element.45), channel_id=1, source_target_pairs={{2,4},{6,0},{4,2},{0,6},{3,5},{7,1},{5,3},{1,7},{10,12},{14,8},{12... | collective-permute-start | bytes 294920 | tf_op jit(solution)/shard_map/ppermute | solution.py:21
  54.6 1.0 %copy-start.7 = (bf16[1,384,384]{2,1,0:T(8,128)(2,1)S(1)}, bf16[1,384,384]{2,1,0:T(8,128)(2,1)}, u32[]{:S(2)}) copy-start(bf16[1,384,384]{2,1,0:T(8,128)(2,1)} %maximum_bitcast_fusion.3) | copy-start | bytes 884740
  54.6 1.0 %copy-start.8 = (bf16[1,384,384]{2,1,0:T(8,128)(2,1)S(1)}, bf16[1,384,384]{2,1,0:T(8,128)(2,1)}, u32[]{:S(2)}) copy-start(bf16[1,384,384]{2,1,0:T(8,128)(2,1)} %maximum_bitcast_fusion.5) | copy-start | bytes 884740
  75.4 0.7 copy-start.3
  76.1 1.0 %copy-start.4 = (f32[16,40,128]{2,1,0:T(8,128)S(1)}, f32[16,40,128]{2,1,0:T(8,128)}, u32[]{:S(2)}) copy-start(f32[16,40,128]{2,1,0:T(8,128)} %copy-done.3) | copy-start | bytes 983044
  (1 other events, 0.7 us)

commit v3 on v2

v3 whole, which is shorter than its diff:
```python
import jax
import jax.numpy as jnp
from jax import lax
from jax.experimental import pallas as pl
from jax.experimental.pallas import tpu as pltpu
from jax.sharding import PartitionSpec as P

STEP_RATIO = 0.4
GRID = ("gx", "gy")
EXACT = lax.Precision.HIGHEST


def shifted(block, axis, distance):
    count = lax.axis_size(axis)
    return lax.ppermute(block, axis, [(i, (i + distance) % count) for i in range(count)])


def swap(upward, downward, axis, parity):
    count = lax.axis_size(axis)
    lows = range(parity, count, 2)
    route = [(i, (i + 1) % count) for i in lows] + [((i + 1) % count, i) for i in lows]
    mine = jnp.where(lax.axis_index(axis) % 2 == parity, upward, downward)
    return lax.ppermute(mine, axis, route)


def exchange(upward, downward, axis):
    if lax.axis_size(axis) % 2:
        return shifted(upward, axis, 1), shifted(downward, axis, -1)
    first, second = swap(upward, downward, axis, 0), swap(upward, downward, axis, 1)
    even = lax.axis_index(axis) % 2 == 0
    return jnp.where(even, second, first), jnp.where(even, first, second)


def everyone(block):
    return spread(jnp.broadcast_to(block[None], (lax.axis_size(GRID),) + block.shape))


def spread(copies):
    return lax.all_to_all(copies, GRID, 0, 0, tiled=True)


def both_halves(rows):
    if lax.axis_size("col") != 2:
        return lax.all_gather(rows, "col", axis=0, tiled=True)
    other = lax.ppermute(rows, "col", [(0, 1), (1, 0)])
    mine_first = lax.axis_index("col") == 0
    return jnp.concatenate([jnp.where(mine_first, rows, other), jnp.where(mine_first, other, rows)])


def halves(solver, leading, face_width):
    swapped = jnp.roll(solver, face_width, axis=1)
    lower = jnp.where(leading == 0, solver[:, :, :face_width], swapped[:, :, face_width:])
    upper = jnp.where(leading == 0, solver[:, :, face_width:], swapped[:, :, :face_width])
    return jnp.concatenate([lower[0], lower[1]], axis=-1), jnp.concatenate([upper[0], upper[1]], axis=-1)


def interface_kernel(out, low_x, high_x, low_y, high_y, below_x, own_x, below_y, own_y, first, second, basis, sums,
                     both, payload):
    rows, face_width = low_x.shape[1], low_x.shape[2]
    pair = 2 * face_width
    lane = lax.broadcasted_iota(jnp.int32, (rows, pair), 1)
    is_first = lane < face_width
    turn = lambda value: pltpu.roll(value, face_width, 1)
    dot = lambda a, b: jnp.dot(a, b, preferred_element_type=jnp.float32)
    kept = basis.shape[1] // 2
    projected = jnp.zeros((kept, rows), jnp.float32)
    sides = ((low_x, high_x, below_x, own_x), (low_y, high_y, below_y, own_y), None)
    for block, side in enumerate(sides):
        at = pl.ds(block * pair, pair)
        mine = out[:, :, at]
        if side is None:
            parts = [turn(mine[c].astype(jnp.float32)) for c in range(2)]
        else:
            low, high, below, own = side
            mine = mine.reshape(2 * rows, pair)
            own_rows = jnp.concatenate([jnp.zeros((face_width, pair), own.dtype), own[:face_width]], axis=0)
            below_rows = jnp.concatenate([below[face_width:], jnp.zeros((face_width, pair), own.dtype)], axis=0)
            ahead = dot(low[...].reshape(2 * rows, face_width), below[:face_width]) + dot(mine, below_rows)
            behind = dot(high[...].reshape(2 * rows, face_width), own[face_width:]) + dot(mine, own_rows)
            parts = [
                jnp.where(is_first, ahead[:rows] - turn(ahead[rows:]), turn(behind[:rows]) - behind[rows:]),
                jnp.where(is_first, turn(ahead[:rows]) + ahead[rows:], behind[:rows] + turn(behind[rows:])),
            ]
        for c in range(2):
            both[c, :, at] = parts[c]
            state = jnp.concatenate([first[c, :, at], second[c, :, at]], axis=0)
            defect = parts[c] - state
            coarser = defect.astype(jnp.bfloat16)
            finer = (defect - coarser.astype(jnp.float32)).astype(jnp.bfloat16)
            fit = lambda a, b: lax.dot_general(a, b, (((1,), (1,)), ((), ())), preferred_element_type=jnp.float32)
            main = fit(basis[c, :, at], coarser)
            projected += main[:kept] + main[kept:] + fit(basis[c, :kept, at], finer)
    tail = jnp.broadcast_to(sums[...], (payload.shape[1] - kept, rows))
    for target in range(payload.shape[0]):
        payload[target, :kept] = projected
        payload[target, kept:] = tail


def solve_interfaces(*args):
    out, basis = args[0], args[11]
    rows, width = out.shape[1:]
    full = pl.BlockSpec(memory_space=pltpu.VMEM)
    return pl.pallas_call(
        interface_kernel,
        in_specs=[full] * len(args),
        out_specs=[full, full],
        out_shape=[
            jax.ShapeDtypeStruct((2, rows, width), jnp.float32),
            jax.ShapeDtypeStruct((lax.axis_size(GRID), basis.shape[1] // 2 + 8, rows), jnp.float32),
        ],
        name="interfaces",
        compiler_params=pltpu.CompilerParams(vmem_limit_bytes=12 * 2**20),
        cost_estimate=pl.CostEstimate(flops=24 * rows * width**2 // 9, bytes_accessed=40 * rows * width, transcendentals=0),
    )(*args)


def per_device(sources, impedance, pair_maps, lead_side, coarse_basis, coarse_inverse):
    drive = sources[0, 0]
    count = drive.shape[1]
    face_width = drive.shape[2] // 6
    basis = coarse_basis[0, 0]
    coarse_count = basis.shape[0]
    face = lambda traces, f: traces[..., f * face_width : (f + 1) * face_width]

    inner_x = lax.axis_index("gx") < lax.axis_size("gx") - 1
    inner_y = lax.axis_index("gy") < lax.axis_size("gy") - 1
    basis_first = basis.transpose(1, 0, 2)
    basis_main = basis_first.astype(jnp.bfloat16)
    basis_split = jnp.concatenate(
        [basis_main, (basis_first - lax.reduce_precision(basis_first, 8, 7)).astype(jnp.bfloat16)], axis=1
    )

    def project(defect):
        return jnp.einsum("csk,pck->ps", defect, basis, precision=EXACT)

    out = [face(drive, f).astype(jnp.bfloat16) for f in range(6)]
    high_y = shifted(out[2], "gy", -1)
    high_x = shifted(out[0], "gx", -1)

    def lower_solves(lower, upper, solver, leading, inside):
        stood_first = leading == 0
        ordered = jnp.where(
            stood_first, jnp.concatenate([lower, upper], axis=-1), jnp.concatenate([upper, lower], axis=-1)
        ).reshape(2 * count, -1)
        real, imag = (jnp.dot(ordered, solver[c], preferred_element_type=jnp.float32) for c in range(2))
        solved = jnp.stack([real[:count] - imag[count:], imag[:count] + real[count:]])
        solved = jnp.where(inside, solved, 0.0)
        head, tail = solved[:, :, :face_width], solved[:, :, face_width:]
        return jnp.where(stood_first, head, tail), jnp.where(stood_first, tail, head)

    face_three, up_y = lower_solves(out[3], high_y, pair_maps[0, 0, 1], lead_side[0, 0, 1], inner_y)
    face_one, up_x = lower_solves(out[1], high_x, pair_maps[0, 0, 0], lead_side[0, 0, 0], inner_x)
    up_y, up_x, solvers_here, part_rows = lax.optimization_barrier((up_y, up_x, pair_maps[0, 0], coarse_inverse))
    own_x, above_x = halves(solvers_here[0], lead_side[0, 0, 0], face_width)
    own_y, above_y = halves(solvers_here[1], lead_side[0, 0, 1], face_width)
    own_x, above_x = (jnp.where(inner_x, m, jnp.zeros_like(m)) for m in (own_x, above_x))
    own_y, above_y = (jnp.where(inner_y, m, jnp.zeros_like(m)) for m in (own_y, above_y))
    below_y, below_x = shifted(above_y, "gy", 1), shifted(above_x, "gx", 1)
    face_two = shifted(up_y, "gy", 1)
    face_zero = shifted(up_x, "gx", 1)
    updated = jnp.concatenate(
        [face_zero, face_one, face_two, face_three, out[5].astype(jnp.float32), out[4].astype(jnp.float32)], axis=-1
    )
    projected = project(updated)
    half = coarse_count // 2
    payload = jnp.concatenate([projected[:half], projected[half:]], axis=1)
    payload, state = lax.optimization_barrier((payload, updated))
    gathered = everyone(payload)
    rows = both_halves(part_rows)

    rounded = jnp.concatenate([state, basis_first], axis=1).astype(jnp.bfloat16)
    total = count + coarse_count
    rounded = rounded.reshape(2 * total, -1)
    first = jnp.dot(rounded, impedance[0, 0, 0], preferred_element_type=jnp.float32)
    second = jnp.dot(rounded, impedance[0, 0, 1], preferred_element_type=jnp.float32)
    product = jnp.stack([first[:total] - second[total:], second[:total] + first[total:]])
    defect_part = jnp.sum(updated * updated, axis=(0, 2))

    gathered = jnp.concatenate([gathered[:, :, :count], gathered[:, :, count:]], axis=1)
    coarse = jnp.einsum("qr,rs->qs", rows, gathered.reshape(-1, count), precision=EXACT)
    correction = jnp.einsum("ps,cpk->csk", coarse, basis_first, precision=EXACT)
    correction_part = jnp.sum(correction * correction, axis=(0, 2))
    response = jnp.einsum("ps,cpk->csk", coarse, product[:, count:], precision=lax.Precision.HIGH)
    outgoing = jnp.concatenate([product[:, :count] + drive, response], axis=1).astype(jnp.bfloat16)
    low_y, high_y = exchange(face(outgoing, 3), face(outgoing, 2), "gy")
    low_x, high_x = exchange(face(outgoing, 1), face(outgoing, 0), "gx")
    sums = jnp.concatenate([defect_part, correction_part])[None]
    both, payload = solve_interfaces(
        outgoing, low_x, high_x, low_y, high_y, below_x, own_x, below_y, own_y, updated, correction, basis_split, sums
    )
    gathered = spread(payload)
    totals = jnp.sum(gathered[:, coarse_count], axis=0)
    factor = STEP_RATIO * jnp.sqrt(totals[:count] / (totals[count:] + 1e-06))
    gathered = gathered[:, :coarse_count]
    gathered = gathered[:, :, :count] + factor * gathered[:, :, count:]
    state = updated + factor[None, :, None] * correction
    updated = both[:, :count] + factor[None, :, None] * both[:, count:]
    defect = updated - state
    coarse = jnp.einsum("qr,rs->qs", rows, gathered.reshape(-1, count), precision=EXACT)
    correction = jnp.einsum("ps,cpk->csk", coarse, basis_first, precision=EXACT)
    sums = jnp.concatenate([jnp.sum(defect * defect, axis=(0, 2)), jnp.sum(correction * correction, axis=(0, 2))])
    totals = jnp.sum(everyone(sums[None]), axis=(0, 1))
    factor = STEP_RATIO * jnp.sqrt(totals[:count] / (totals[count:] + 1e-06))
    iterate = updated + factor[None, :, None] * correction
    return iterate[None, None]


def solution(mesh):
    return jax.shard_map(
        per_device,
        mesh=mesh,
        in_specs=(
            P("gx", "gy", None, "col", None),
            P("gx", "gy", None, None, None),
            P("gx", "gy", None, None, None, None),
            P("gx", "gy", None),
            P("gx", "gy", None, None, None),
            P(("gx", "gy", "col"), None),
        ),
        out_specs=P("gx", "gy", None, "col", None),
        check_vma=False,
    )
```

time: 89.8 us -> 89 us (level)
  waiting for transfers between devices: 13 us -> 19 us
  other arithmetic: 14.6 us -> 10.5 us
  local copies, waits for them, and re-layouts: 8.87 us -> 5.18 us
  Pallas kernels: 0 us -> 1.65 us
  matrix products: 12.9 us -> 11.9 us
    ppermute x4, waiting for transfers between devices: 2.72 us -> 11.1 us  [swap(): return lax.ppermute(mine, axis, route)]
    ppermute x6, waiting for transfers between devices: 6.7 us -> 1.75 us  [shifted(): lax.ppermute(block, axis, [(i, (i + distance) % count) for i in range(cou...]
    concatenate x12 -> x4, other arithmetic: 4.13 us -> 0.13 us  [the longest x1 0.05 us: per_device(): jnp.concatenate([product[:, :count] + drive, response], axis=1)]
    select_n x0 -> x7, other arithmetic: none -> 2.71 us  [the longest x2 0.96 us: per_device(): jnp.where(inner_y, m, jnp.zeros_like(m))]
    all_to_all x1, waiting for transfers between devices: 3.53 us -> 6.11 us  [spread(): return lax.all_to_all(copies, GRID, 0, 0, tiled=True)]
    slice x8 -> x3, local copies, waits for them, and re-layouts: 3.12 us -> 0.77 us  [the longest x1 0.65 us: per_device(): lead_side[0, 0, 0]]
    unnamed x27 -> x21, local copies, waits for them, and re-layouts: 3.02 us -> 1.08 us
    pallas_call x0 -> x1, Pallas kernels: none -> 1.65 us  [solve_interfaces(): pl.pallas_call(interface_kernel, in_specs=[full] * len(args), out_specs=[...]
  transfers between devices with their start and end apart: 12 -> 12, of which waited for: 5 -> 4; matrix products, arithmetic and copies ran while one was open for 16% -> 23% of each run, Pallas kernels for 0% -> 0%
where the time goes in v3:
time: 89 us; the launch traced here: 88.4 us
  blocking collectives  23.1 us (26%)
  waiting for transfers between devices  19 us (21%)
  starting transfers between devices  15.4 us (17%)
  matrix products  11.9 us (13%)
  other arithmetic  10.5 us (12%)
  local copies, waits for them, and re-layouts  5.18 us (6%)
  between operations  1.73 us (2%)
  Pallas kernels  1.65 us (2%)
    all_to_all x2, blocking collectives, spread(): return lax.all_to_all(copies, GRID, 0, 0, tiled=True)  23.1 us
    ppermute x4, waiting for transfers between devices, swap(): return lax.ppermute(mine, axis, route)  11.1 us
    ppermute x6, starting transfers between devices, shifted(): lax.ppermute(block, axis, [(i, (i + distance) % count) for i in range(cou...  7.84 us
    all_to_all x1, waiting for transfers between devices, spread(): return lax.all_to_all(copies, GRID, 0, 0, tiled=True)  6.11 us
    all_to_all x1, starting transfers between devices, spread(): return lax.all_to_all(copies, GRID, 0, 0, tiled=True)  4.17 us
    dot_general x1, matrix products, per_device(): jnp.dot(rounded, impedance[0, 0, 0], preferred_element_type=jnp.float32)  3.49 us
    dot_general x1, matrix products, per_device(): jnp.dot(rounded, impedance[0, 0, 1], preferred_element_type=jnp.float32)  3.47 us
    ppermute x4, starting transfers between devices, swap(): return lax.ppermute(mine, axis, route)  1.93 us
  transfers between devices with their start and end apart: 12, of which 4 were waited for; matrix products, arithmetic and copies ran while one was open for 23% of the time, Pallas kernels for 0%

profile of v3, /device:TPU:0, one launch (start us, length us, event | category | flops | bytes accessed | tf_op | source)
XLA Modules:
  0.0 88.4 jit_solution(9721302816766999019)
XLA Ops:
  0.0 1.1 %bitcast_convert_fusion = bf16[2,64,1152]{2,1,0:T(8,128)(2,1)S(1)} fusion(f32[1,1,2,64,1152]{4,3,2,1,0:T(8,128)} %param.6), kind=kLoop, calls=%fused_computation.32 | loop fusion | flops 147456 | bytes 884736 | tf_op jit(solution)/shard_map/convert.10
  1.2 0.8 slice_convert_fusion
  1.9 5.1 %collective-permute-start.1 = (bf16[2,64,192]{2,1,0:T(8,128)(2,1)S(1)}, bf16[2,64,192]{2,1,0:T(8,128)(2,1)S(1)}, u32[]{:S(2)}, u32[]{:S(2)}) collective-permute-start(bf16[2,64,192]{2,1,0:T(8,128)(2,1)S(1)} %get-tuple-element.51), channel_id=1, source_target_pairs={{0,24},{8,0},{16,8},{24,16},{1,25},{9,1},{17,9},{25,17},{2,26},{10... | collective-permute-start | bytes 147464 | tf_op jit(solution)/shard_map/ppermute | solution.py:15
  11.1 0.8 slice_select_fusion
  11.9 1.5 %collective-permute-start.4 = (f32[16,512]{1,0:T(8,128)S(1)}, f32[16,512]{1,0:T(8,128)S(1)}, u32[]{:S(2)}, u32[]{:S(2)}) collective-permute-start(f32[16,512]{1,0:T(8,128)S(1)} %copy-done.8), channel_id=1, source_target_pairs={{0,1},{1,0},{2,3},{3,2},{4,5},{5,4},{6,7},{7,6},{8,9},{9,8},{10,11... | collective-permute-start | bytes 98312 | tf_op jit(solution)/shard_map/ppermute | solution.py:45
  14.6 0.8 maximum_select_fusion.2
  16.5 0.8 maximum_select_fusion
  17.3 1.1 %collective-permute-start.9 = (bf16[384,384]{1,0:T(8,128)(2,1)}, bf16[384,384]{1,0:T(8,128)(2,1)S(1)}, u32[]{:S(2)}, u32[]{:S(2)}) collective-permute-start(bf16[384,384]{1,0:T(8,128)(2,1)} %maximum_select_fusion), channel_id=1, source_target_pairs={{0,8},{8,16},{16,24},{24,0},{1,9},{9,17},{17,25},{25,1},{2,10},{10... | collective-permute-start | bytes 884744 | tf_op jit(solution)/shard_map/ppermute | solution.py:15
  19.4 1.7 %collective-permute-done.2 = f32[2,64,192]{2,1,0:T(8,128)S(1)} collective-permute-done((f32[2,64,192]{2,1,0:T(8,128)S(1)}, f32[2,64,192]{2,1,0:T(8,128)S(1)}, u32[]{:S(2)}, u32[]{:S(2)}) %collective-permute-start.2) | collective-permute-done | bytes 98336 | tf_op jit(solution)/shard_map/ppermute | solution.py:15
  21.8 1.4 %concatenate.80.first = f32[2,64,1152]{2,1,0:T(8,128)S(1)} concatenate(f32[2,64,192]{2,1,0:T(8,128)} %copy-done.6, f32[2,64,192]{2,1,0:T(8,128)} %get-tuple-element.61, f32[2,64,192]{2,1,0:T(8,128)} %copy-done.7, f32[2,64,192]{2,1,0:T(8,128)} %get-tuple-element.76, f32[2,64,192]{2,1,0:T(8,128)} %get-tuple-element.50, f32[2,64,192]{2,1,0:T(8,128)S(1)} %get-tuple-element.49), dimensions={2} | concatenate | bytes 1179648 | tf_op jit(solution)/shard_map/concatenate | solution.py:161
  24.0 3.5 %fusion = f32[192,1152]{1,0:T(8,128)} fusion(bf16[192,1152]{1,0:T(8,128)(2,1)S(1)} %bitcast.113, bf16[1,1,2,1152,1152]{4,3,2,1,0:T(8,128)(2,1)} %param.7), kind=kOutput, calls=%fused_computation | convolution fusion | flops 509607936 | bytes 3981312 | tf_op jit(solution)/shard_map/dot_general | solution.py:175
  27.5 3.5 %fusion.2 = f32[192,1152]{1,0:T(8,128)} fusion(bf16[192,1152]{1,0:T(8,128)(2,1)S(1)} %bitcast.114, bf16[1,1,2,1152,1152]{4,3,2,1,0:T(8,128)(2,1)} %param.7), kind=kOutput, calls=%fused_computation.2 | convolution fusion | flops 509607936 | bytes 3981312 | tf_op jit(solution)/shard_map/dot_general | solution.py:174
  31.6 4.2 %all-to-all-start = ((f32[16,16,128]{2,1,0:T(8,128)}), f32[16,16,128]{2,1,0:T(8,128)}, u32[]{:S(2)}, u32[]{:S(2)}) async-start(f32[16,16,128]{2,1,0:T(8,128)} %broadcast_in_dim.14), calls=%async_computation | async-start | bytes 262144 | tf_op jit(solution)/shard_map/all_to_all | solution.py:39
  35.8 1.6 %fusion.12 = (f32[1,96,1152]{2,1,0:T(8,128)S(1)}, f32[1,96,1152]{2,1,0:T(8,128)S(1)}) fusion(f32[192,1152]{1,0:T(8,128)} %fusion, f32[192,1152]{1,0:T(8,128)} %fusion.2), kind=kLoop, calls=%fused_computation.43 | loop fusion | flops 221184 | bytes 2654208 | tf_op jit(solution)/shard_map/stack | solution.py:176
  37.6 6.1 %all-to-all-done = f32[16,16,128]{2,1,0:T(8,128)} async-done(((f32[16,16,128]{2,1,0:T(8,128)}), f32[16,16,128]{2,1,0:T(8,128)}, u32[]{:S(2)}, u32[]{:S(2)}) %all-to-all-start) | async-done | bytes 131104 | tf_op jit(solution)/shard_map/all_to_all | solution.py:39
  43.7 1.1 %fusion.58 = (f32[16,16,64]{2,1,0:T(8,128)S(1)}, f32[16,16,64]{2,1,0:T(8,128)S(1)}) fusion(f32[16,16,128]{2,1,0:T(8,128)} %all-to-all-done), kind=kLoop, calls=%fused_computation.143 | loop fusion | bytes 262144 | tf_op jit(solution)/shard_map/slice | solution.py:179
  44.8 1.0 %convolution_bitcast_fusion.2 = f32[32,64,1]{1,0,2:T(8,128)S(1)} fusion(f32[512,64]{1,0:T(8,128)S(1)} %bitcast.111, f32[16,512]{1,0:T(8,128)} %get-tuple-element.66, f32[16,512]{1,0:T(8,128)} %get-tuple-element.65), kind=kOutput, calls=%fused_computation.10 | convolution fusion | flops 12599296 | bytes 204800 | tf_op jit(solution)/shard_map/qr,rs->qs/dot_general | solution.py:180
  47.5 1.8 %collective-permute-start.5 = (bf16[2,128,192]{2,1,0:T(8,128)(2,1)S(1)}, bf16[2,128,192]{2,1,0:T(8,128)(2,1)S(1)}, u32[]{:S(2)}, u32[]{:S(2)}) collective-permute-start(bf16[2,128,192]{2,1,0:T(8,128)(2,1)S(1)} %get-tuple-element.35), channel_id=1, source_target_pairs={{8,16},{24,0},{16,8},{0,24},{9,17},{25,1},{17,9},{1,25},{10,18},{2... | collective-permute-start | bytes 294920 | tf_op jit(solution)/shard_map/ppermute | solution.py:23
  49.4 6.8 %collective-permute-done.6 = bf16[2,128,192]{2,1,0:T(8,128)(2,1)S(1)} collective-permute-done((bf16[2,128,192]{2,1,0:T(8,128)(2,1)S(1)}, bf16[2,128,192]{2,1,0:T(8,128)(2,1)S(1)}, u32[]{:S(2)}, u32[]{:S(2)}) %collective-permute-start.6) | collective-permute-done | bytes 98336 | tf_op jit(solution)/shard_map/ppermute | solution.py:23
  56.2 4.3 %collective-permute-done.7 = bf16[2,128,192]{2,1,0:T(8,128)(2,1)S(1)} collective-permute-done((bf16[2,128,192]{2,1,0:T(8,128)(2,1)S(1)}, bf16[2,128,192]{2,1,0:T(8,128)(2,1)S(1)}, u32[]{:S(2)}, u32[]{:S(2)}) %collective-permute-start.7) | collective-permute-done | bytes 98336 | tf_op jit(solution)/shard_map/ppermute | solution.py:23
  60.6 1.7 %interfaces.1 = (f32[2,128,1152]{2,1,0:T(8,128)S(1)}, f32[16,40,128]{2,1,0:T(8,128)S(1)}) custom-call(bf16[2,128,1152]{2,1,0:T(8,128)(2,1)S(1)} %pad_maximum_fusion.out, bf16[2,128,192]{2,1,0:T(8,128)(2,1)S(1)} %get-tuple-element.58.low_x, bf16[2,128,192]{2,1,0:T(8,128)(2,1)S(1)} %get-tuple-element.57.high_x, ...), custom_call_target="tpu_custom_call" | custom-call | flops 452984832 | bytes 5898240 | tf_op jit(solution)/shard_map/interfaces/pallas_call | solution.py:103
  62.3 13.7 %all_to_all.15 = f32[16,40,128]{2,1,0:T(8,128)S(1)} all-to-all(f32[16,40,128]{2,1,0:T(8,128)S(1)} %get-tuple-element.20), channel_id=1, replica_groups=mesh['gx'=4,'gy'=4,'col'=2] {'gx','gy'}, dimensions={0} | all-to-all | bytes 655360 | tf_op jit(solution)/shard_map/all_to_all | solution.py:39
  78.0 9.4 %all_to_all.16 = f32[16,1,128]{2,1,0:T(1,128)S(1)} all-to-all(f32[16,1,128]{2,1,0:T(1,128)S(1)} %broadcast_in_dim.29), channel_id=1, replica_groups=mesh['gx'=4,'gy'=4,'col'=2] {'gx','gy'}, dimensions={0} | all-to-all | bytes 16384 | tf_op jit(solution)/shard_map/all_to_all | solution.py:39
  87.4 1.0 %fusion.10 = f32[1,1,2,64,1152]{4,3,2,1,0:T(8,128)} fusion(f32[64,2,1152]{2,0,1:T(8,128)S(1)} %get-tuple-element.74, f32[64]{0:T(128)S(1)} %sqrt_multiply_fusion, f32[2,128,1152]{2,1,0:T(8,128)S(1)} %get-tuple-element.19, f32[64]{0:T(128)S(1)} %sqrt_multiply_fusion.1), kind=kLoop, calls=%fused_computation.31 | loop fusion | flops 589824 | bytes 2359808 | tf_op jit(solution)/shard_map/broadcast_in_dim | solution.py:205
  (85 shorter events, 12.0 us)
Async XLA Ops:
  0.0 7.7 %copy-start = (f32[1,1,32,2,1152]{4,3,2,1,0:T(2,128)S(1)}, f32[1,1,32,2,1152]{4,3,2,1,0:T(2,128)}, u32[]{:S(2)}) copy-start(f32[1,1,32,2,1152]{4,3,2,1,0:T(2,128)} %param.10) | copy-start | bytes 884740
  1.1 6.7 %copy-start.9 = (s32[1,1,2]{2,1,0:T(1,128)S(1)}, s32[1,1,2]{2,1,0:T(1,128)}, u32[]{:S(2)}) copy-start(s32[1,1,2]{2,1,0:T(1,128)} %param.9) | copy-start | bytes 28
  1.2 8.6 %copy-start.2 = (bf16[1,1,2,2,384,384]{5,4,3,2,1,0:T(8,128)(2,1)S(1)}, bf16[1,1,2,2,384,384]{5,4,3,2,1,0:T(8,128)(2,1)}, u32[]{:S(2)}) copy-start(bf16[1,1,2,2,384,384]{5,4,3,2,1,0:T(8,128)(2,1)} %param.8) | copy-start | bytes 3538948
  1.9 8.4 %collective-permute-start.1 = (bf16[2,64,192]{2,1,0:T(8,128)(2,1)S(1)}, bf16[2,64,192]{2,1,0:T(8,128)(2,1)S(1)}, u32[]{:S(2)}, u32[]{:S(2)}) collective-permute-start(bf16[2,64,192]{2,1,0:T(8,128)(2,1)S(1)} %get-tuple-element.51), channel_id=1, source_target_pairs={{0,24},{8,0},{16,8},{24,16},{1,25},{9,1},{17,9},{25,17},{2,26},{10... | collective-permute-start | bytes 147464 | tf_op jit(solution)/shard_map/ppermute | solution.py:15
  7.0 2.8 %collective-permute-start = (bf16[2,64,192]{2,1,0:T(8,128)(2,1)S(1)}, bf16[2,64,192]{2,1,0:T(8,128)(2,1)S(1)}, u32[]{:S(2)}, u32[]{:S(2)}) collective-permute-start(bf16[2,64,192]{2,1,0:T(8,128)(2,1)S(1)} %get-tuple-element.53), channel_id=1, source_target_pairs={{0,6},{2,0},{4,2},{6,4},{1,7},{3,1},{5,3},{7,5},{8,14},{10,8},{12,... | collective-permute-start | bytes 147464 | tf_op jit(solution)/shard_map/ppermute | solution.py:15
  11.0 0.9 %copy-start.8 = (f32[16,512]{1,0:T(8,128)S(1)}, f32[16,512]{1,0:T(8,128)}, u32[]{:S(2)}) copy-start(f32[16,512]{1,0:T(8,128)} %param.11) | copy-start | bytes 98308
  11.0 2.9 %copy-start.3 = (bf16[1,1,2,2,384,384]{5,4,3,2,1,0:T(8,128)(2,1)S(1)}, bf16[1,1,2,2,384,384]{5,4,3,2,1,0:T(8,128)(2,1)}, u32[]{:S(2)}) copy-start(bf16[1,1,2,2,384,384]{5,4,3,2,1,0:T(8,128)(2,1)} %param.8) | copy-start | bytes 3538948
  11.9 6.8 %collective-permute-start.4 = (f32[16,512]{1,0:T(8,128)S(1)}, f32[16,512]{1,0:T(8,128)S(1)}, u32[]{:S(2)}, u32[]{:S(2)}) collective-permute-start(f32[16,512]{1,0:T(8,128)S(1)} %copy-done.8), channel_id=1, source_target_pairs={{0,1},{1,0},{2,3},{3,2},{4,5},{5,4},{6,7},{7,6},{8,9},{9,8},{10,11... | collective-permute-start | bytes 98312 | tf_op jit(solution)/shard_map/ppermute | solution.py:45
  13.4 7.7 %collective-permute-start.2 = (f32[2,64,192]{2,1,0:T(8,128)S(1)}, f32[2,64,192]{2,1,0:T(8,128)S(1)}, u32[]{:S(2)}, u32[]{:S(2)}) collective-permute-start(f32[2,64,192]{2,1,0:T(8,128)S(1)} %get-tuple-element.13), channel_id=1, source_target_pairs={{0,8},{8,16},{16,24},{24,0},{1,9},{9,17},{17,25},{25,1},{2,10},{10... | collective-permute-start | bytes 294920 | tf_op jit(solution)/shard_map/ppermute | solution.py:15
  13.4 7.7 %collective-permute-start.3 = (f32[2,64,192]{2,1,0:T(8,128)S(1)}, f32[2,64,192]{2,1,0:T(8,128)S(1)}, u32[]{:S(2)}, u32[]{:S(2)}) collective-permute-start(f32[2,64,192]{2,1,0:T(8,128)S(1)} %get-tuple-element.14), channel_id=1, source_target_pairs={{0,2},{2,4},{4,6},{6,0},{1,3},{3,5},{5,7},{7,1},{8,10},{10,12},{12... | collective-permute-start | bytes 294920 | tf_op jit(solution)/shard_map/ppermute | solution.py:15
  15.5 45.1 %collective-permute-start.10 = (bf16[384,384]{1,0:T(8,128)(2,1)}, bf16[384,384]{1,0:T(8,128)(2,1)S(1)}, u32[]{:S(2)}, u32[]{:S(2)}) collective-permute-start(bf16[384,384]{1,0:T(8,128)(2,1)} %maximum_select_fusion.2), channel_id=1, source_target_pairs={{0,2},{2,4},{4,6},{6,0},{1,3},{3,5},{5,7},{7,1},{8,10},{10,12},{12... | collective-permute-start | bytes 884744 | tf_op jit(solution)/shard_map/ppermute | solution.py:15
  17.3 43.3 %collective-permute-start.9 = (bf16[384,384]{1,0:T(8,128)(2,1)}, bf16[384,384]{1,0:T(8,128)(2,1)S(1)}, u32[]{:S(2)}, u32[]{:S(2)}) collective-permute-start(bf16[384,384]{1,0:T(8,128)(2,1)} %maximum_select_fusion), channel_id=1, source_target_pairs={{0,8},{8,16},{16,24},{24,0},{1,9},{9,17},{17,25},{25,1},{2,10},{10... | collective-permute-start | bytes 884744 | tf_op jit(solution)/shard_map/ppermute | solution.py:15
  21.1 0.7 copy-start.6
  21.1 0.7 copy-start.7
  31.6 12.1 %all-to-all-start = ((f32[16,16,128]{2,1,0:T(8,128)}), f32[16,16,128]{2,1,0:T(8,128)}, u32[]{:S(2)}, u32[]{:S(2)}) async-start(f32[16,16,128]{2,1,0:T(8,128)} %broadcast_in_dim.14), calls=%async_computation | async-start | bytes 262144 | tf_op jit(solution)/shard_map/all_to_all | solution.py:39
  35.8 1.6 %copy-start.1 = (f32[1,1,2,64,1152]{4,3,2,1,0:T(8,128)S(1)}, f32[1,1,2,64,1152]{4,3,2,1,0:T(8,128)}, u32[]{:S(2)}) copy-start(f32[1,1,2,64,1152]{4,3,2,1,0:T(8,128)} %param.6) | copy-start | bytes 1769476
  47.4 8.8 %collective-permute-start.8 = (bf16[2,128,192]{2,1,0:T(8,128)(2,1)S(1)}, bf16[2,128,192]{2,1,0:T(8,128)(2,1)S(1)}, u32[]{:S(2)}, u32[]{:S(2)}) collective-permute-start(bf16[2,128,192]{2,1,0:T(8,128)(2,1)S(1)} %get-tuple-element.33), channel_id=1, source_target_pairs={{0,2},{4,6},{2,0},{6,4},{1,3},{5,7},{3,1},{7,5},{8,10},{12,14},{10... | collective-permute-start | bytes 294920 | tf_op jit(solution)/shard_map/ppermute | solution.py:23
  47.5 8.7 %collective-permute-start.6 = (bf16[2,128,192]{2,1,0:T(8,128)(2,1)S(1)}, bf16[2,128,192]{2,1,0:T(8,128)(2,1)S(1)}, u32[]{:S(2)}, u32[]{:S(2)}) collective-permute-start(bf16[2,128,192]{2,1,0:T(8,128)(2,1)S(1)} %get-tuple-element.34), channel_id=1, source_target_pairs={{0,8},{16,24},{8,0},{24,16},{1,9},{17,25},{9,1},{25,17},{2,10},{18... | collective-permute-start | bytes 294920 | tf_op jit(solution)/shard_map/ppermute | solution.py:23
  47.5 8.6 %collective-permute-start.5 = (bf16[2,128,192]{2,1,0:T(8,128)(2,1)S(1)}, bf16[2,128,192]{2,1,0:T(8,128)(2,1)S(1)}, u32[]{:S(2)}, u32[]{:S(2)}) collective-permute-start(bf16[2,128,192]{2,1,0:T(8,128)(2,1)S(1)} %get-tuple-element.35), channel_id=1, source_target_pairs={{8,16},{24,0},{16,8},{0,24},{9,17},{25,1},{17,9},{1,25},{10,18},{2... | collective-permute-start | bytes 294920 | tf_op jit(solution)/shard_map/ppermute | solution.py:23
  56.2 4.4 %collective-permute-start.7 = (bf16[2,128,192]{2,1,0:T(8,128)(2,1)S(1)}, bf16[2,128,192]{2,1,0:T(8,128)(2,1)S(1)}, u32[]{:S(2)}, u32[]{:S(2)}) collective-permute-start(bf16[2,128,192]{2,1,0:T(8,128)(2,1)S(1)} %get-tuple-element.36), channel_id=1, source_target_pairs={{2,4},{6,0},{4,2},{0,6},{3,5},{7,1},{5,3},{1,7},{10,12},{14,8},{12... | collective-permute-start | bytes 294920 | tf_op jit(solution)/shard_map/ppermute | solution.py:23
  76.1 0.8 copy-start.4
  76.1 0.8 copy-start.5

commit v4 on v3

--- a/solution.py
+++ b/solution.py
@@ -17,15 +17,14 @@
 
 def swap(upward, downward, axis, parity):
     count = lax.axis_size(axis)
-    lows = range(parity, count, 2)
-    route = [(i, (i + 1) % count) for i in lows] + [((i + 1) % count, i) for i in lows]
+    partner = list(range(count))
+    for low in range(parity, count - 1, 2):
+        partner[low], partner[low + 1] = low + 1, low
     mine = jnp.where(lax.axis_index(axis) % 2 == parity, upward, downward)
-    return lax.ppermute(mine, axis, route)
+    return lax.ppermute(mine, axis, list(enumerate(partner)))
 
 
 def exchange(upward, downward, axis):
-    if lax.axis_size(axis) % 2:
-        return shifted(upward, axis, 1), shifted(downward, axis, -1)
     first, second = swap(upward, downward, axis, 0), swap(upward, downward, axis, 1)
     even = lax.axis_index(axis) % 2 == 0
     return jnp.where(even, second, first), jnp.where(even, first, second)
@@ -96,6 +95,87 @@
         payload[target, kept:] = tail
 
 
+def fit(a, b):
+    return lax.dot_general(a, b, (((1,), (1,)), ((), ())), preferred_element_type=jnp.float32)
+
+
+def parted(value):
+    coarser = value.astype(jnp.bfloat16)
+    return coarser, (value - coarser.astype(jnp.float32)).astype(jnp.bfloat16)
+
+
+def row_sums(squares):
+    coarser, finer = parted(squares)
+    ones = jnp.ones((16, squares.shape[1]), jnp.bfloat16)
+    return (fit(ones, coarser) + fit(ones, finer))[:1]
+
+
+def join_kernel(zero, one, two, three, four, five, basis, updated, payload, norms):
+    count, face_width = zero.shape[1], zero.shape[2]
+    kept, pair = basis.shape[1] // 2, 2 * face_width
+    projected = jnp.zeros((kept, 2 * count), jnp.float32)
+    squares = jnp.zeros((count, pair), jnp.float32)
+    for block, (low, high) in enumerate(((zero, one), (two, three), (five, four))):
+        at = pl.ds(block * pair, pair)
+        for c in range(2):
+            updated[c, :, block * pair : block * pair + face_width] = low[c].astype(jnp.float32)
+            updated[c, :, block * pair + face_width : (block + 1) * pair] = high[c].astype(jnp.float32)
+            value = updated[c, :, at]
+            squares += value * value
+            coarser, finer = parted(jnp.concatenate([value, value], axis=0))
+            main = fit(basis[c, :, at], coarser)
+            projected += main[:kept] + main[kept:] + fit(basis[c, :kept, at], finer)
+    norms[...] = row_sums(squares)
+    lane = lax.broadcasted_iota(jnp.int32, (kept // 2, 2 * count), 1)
+    packed = jnp.where(lane < count, projected[: kept // 2], projected[kept // 2 :])
+    for target in range(payload.shape[0]):
+        payload[target] = packed
+
+
+def correct_kernel(gathered, rows, basis, products, drive, norms, correction, outgoing, sums):
+    count, kept = drive.shape[1], basis.shape[1]
+    total, width = count + kept, drive.shape[2]
+    pieces = []
+    for n in range(gathered.shape[0]):
+        block = gathered[n]
+        pieces += [block[:, :count], pltpu.roll(block, count, 1)[:, :count]]
+    coarse = jnp.dot(
+        rows[...], jnp.concatenate(pieces, axis=0), precision=EXACT, preferred_element_type=jnp.float32
+    ).T
+    major, minor = parted(coarse)
+    weights = jnp.concatenate([major, major, minor], axis=1)
+
+    def combined(vectors):
+        upper, lower = parted(vectors)
+        return jnp.dot(weights, jnp.concatenate([upper, lower, upper], axis=0), preferred_element_type=jnp.float32)
+
+    squares = jnp.zeros((count, width), jnp.float32)
+    for c in range(2):
+        value = combined(basis[c])
+        correction[c] = value
+        squares += value * value
+        if c == 0:
+            product = products[0, :total] - products[1, total:]
+        else:
+            product = products[1, :total] + products[0, total:]
+        outgoing[c, :count] = (product[:count] + drive[c]).astype(jnp.bfloat16)
+        outgoing[c, count:] = combined(product[count:]).astype(jnp.bfloat16)
+    sums[...] = jnp.concatenate([norms[...], row_sums(squares)], axis=1)
+
+
+def on_chip(kernel, out_shape, flops, *args):
+    full = pl.BlockSpec(memory_space=pltpu.VMEM)
+    moved = sum(a.size * a.dtype.itemsize for a in args)
+    return pl.pallas_call(
+        kernel,
+        in_specs=[full] * len(args),
+        out_specs=[full] * len(out_shape),
+        out_shape=out_shape,
+        compiler_params=pltpu.CompilerParams(vmem_limit_bytes=12 * 2**20),
+        cost_estimate=pl.CostEstimate(flops=flops, bytes_accessed=moved, transcendentals=0),
+    )(*args)
+
+
 def solve_interfaces(*args):
     out, basis = args[0], args[11]
     rows, width = out.shape[1:]
@@ -130,9 +210,6 @@
         [basis_main, (basis_first - lax.reduce_precision(basis_first, 8, 7)).astype(jnp.bfloat16)], axis=1
     )
 
-    def project(defect):
-        return jnp.einsum("csk,pck->ps", defect, basis, precision=EXACT)
-
     out = [face(drive, f).astype(jnp.bfloat16) for f in range(6)]
     high_y = shifted(out[2], "gy", -1)
     high_x = shifted(out[0], "gx", -1)
@@ -158,33 +235,37 @@
     below_y, below_x = shifted(above_y, "gy", 1), shifted(above_x, "gx", 1)
     face_two = shifted(up_y, "gy", 1)
     face_zero = shifted(up_x, "gx", 1)
-    updated = jnp.concatenate(
-        [face_zero, face_one, face_two, face_three, out[5].astype(jnp.float32), out[4].astype(jnp.float32)], axis=-1
-    )
-    projected = project(updated)
-    half = coarse_count // 2
-    payload = jnp.concatenate([projected[:half], projected[half:]], axis=1)
+    groups = lax.axis_size(GRID)
+    updated, payload, defect_part = on_chip(
+        join_kernel,
+        [
+            jax.ShapeDtypeStruct(drive.shape, jnp.float32),
+            jax.ShapeDtypeStruct((groups, coarse_count // 2, 2 * count), jnp.float32),
+            jax.ShapeDtypeStruct((1, count), jnp.float32),
+        ],
+        12 * coarse_count * count * drive.shape[2],
+        face_zero, face_one, face_two, face_three, out[4], out[5], basis_split,
+    )
     payload, state = lax.optimization_barrier((payload, updated))
-    gathered = everyone(payload)
+    gathered = spread(payload)
     rows = both_halves(part_rows)
 
     rounded = jnp.concatenate([state, basis_first], axis=1).astype(jnp.bfloat16)
     total = count + coarse_count
     rounded = rounded.reshape(2 * total, -1)
-    first = jnp.dot(rounded, impedance[0, 0, 0], preferred_element_type=jnp.float32)
-    second = jnp.dot(rounded, impedance[0, 0, 1], preferred_element_type=jnp.float32)
-    product = jnp.stack([first[:total] - second[total:], second[:total] + first[total:]])
-    defect_part = jnp.sum(updated * updated, axis=(0, 2))
-
-    gathered = jnp.concatenate([gathered[:, :, :count], gathered[:, :, count:]], axis=1)
-    coarse = jnp.einsum("qr,rs->qs", rows, gathered.reshape(-1, count), precision=EXACT)
-    correction = jnp.einsum("ps,cpk->csk", coarse, basis_first, precision=EXACT)
-    correction_part = jnp.sum(correction * correction, axis=(0, 2))
-    response = jnp.einsum("ps,cpk->csk", coarse, product[:, count:], precision=lax.Precision.HIGH)
-    outgoing = jnp.concatenate([product[:, :count] + drive, response], axis=1).astype(jnp.bfloat16)
+    products = jnp.einsum("rk,ckm->crm", rounded, impedance[0, 0], preferred_element_type=jnp.float32)
+    correction, outgoing, sums = on_chip(
+        correct_kernel,
+        [
+            jax.ShapeDtypeStruct(drive.shape, jnp.float32),
+            jax.ShapeDtypeStruct((2, 2 * count, drive.shape[2]), jnp.bfloat16),
+            jax.ShapeDtypeStruct((1, 2 * count), jnp.float32),
+        ],
+        24 * coarse_count * count * drive.shape[2],
+        gathered, rows, basis_first, products, drive, defect_part,
+    )
     low_y, high_y = exchange(face(outgoing, 3), face(outgoing, 2), "gy")
     low_x, high_x = exchange(face(outgoing, 1), face(outgoing, 0), "gx")
-    sums = jnp.concatenate([defect_part, correction_part])[None]
     both, payload = solve_interfaces(
         outgoing, low_x, high_x, low_y, high_y, below_x, own_x, below_y, own_y, updated, correction, basis_split, sums
     )

time: 89 us -> 78.1 us (0.88)
  waiting for transfers between devices: 19 us -> 7.87 us
  blocking collectives: 23.1 us -> 29.3 us
  matrix products: 11.9 us -> 6.03 us
  Pallas kernels: 1.65 us -> 6.13 us
  other arithmetic: 10.5 us -> 7.64 us
  local copies, waits for them, and re-layouts: 5.18 us -> 3.04 us
    ppermute x4, waiting for transfers between devices: 11.1 us -> 3.92 us  [swap(): return lax.ppermute(mine, axis, list(enumerate(partner)))]
    all_to_all x2, blocking collectives: 23.1 us -> 29.3 us  [spread(): return lax.all_to_all(copies, GRID, 0, 0, tiled=True)]
    dot_general x4 -> x1, matrix products: 8.01 us -> 3.9 us  [per_device(): jnp.einsum('rk,ckm->crm', rounded, impedance[0, 0], preferred_element_typ...]
    pallas_call x0 -> x2, Pallas kernels: none -> 3.41 us  [on_chip(): pl.pallas_call(kernel, in_specs=[full] * len(args), out_specs=[full] * le...]
    all_to_all x1, waiting for transfers between devices: 6.11 us -> 3.93 us  [spread(): return lax.all_to_all(copies, GRID, 0, 0, tiled=True)]
    ppermute x6, waiting for transfers between devices: 1.75 us -> 0.02 us  [shifted(): lax.ppermute(block, axis, [(i, (i + distance) % count) for i in range(cou...]
    another operation x4 -> x2, other arithmetic: 2.8 us -> 1.18 us  [the longest x1 1.57 us: per_device(): jnp.stack([first[:total] - second[total:], second[:total] + first[total:]])]
    concatenate x1 -> x0, local copies, waits for them, and re-layouts: 1.37 us -> none  [per_device(): jnp.concatenate([face_zero, face_one, face_two, face_three, out[5].astype...]
  transfers between devices with their start and end apart: 12 -> 12, of which waited for: 4 -> 2; matrix products, arithmetic and copies ran while one was open for 23% -> 14% of each run, Pallas kernels for 0% -> 4%
where the time goes in v4:
time: 78.1 us; the launch traced here: 77.6 us
  blocking collectives  29.3 us (38%)
  starting transfers between devices  15.7 us (20%)
  waiting for transfers between devices  7.87 us (10%)
  other arithmetic  7.64 us (10%)
  Pallas kernels  6.13 us (8%)
  matrix products  6.03 us (8%)
  local copies, waits for them, and re-layouts  3.04 us (4%)
  between operations  1.84 us (2%)
    all_to_all x2, blocking collectives, spread(): return lax.all_to_all(copies, GRID, 0, 0, tiled=True)  29.3 us
    ppermute x6, starting transfers between devices, shifted(): lax.ppermute(block, axis, [(i, (i + distance) % count) for i in range(cou...  7.67 us
    all_to_all x1, starting transfers between devices, spread(): return lax.all_to_all(copies, GRID, 0, 0, tiled=True)  4.97 us
    all_to_all x1, waiting for transfers between devices, spread(): return lax.all_to_all(copies, GRID, 0, 0, tiled=True)  3.93 us
    ppermute x4, waiting for transfers between devices, swap(): return lax.ppermute(mine, axis, list(enumerate(partner)))  3.92 us
    dot_general x1, matrix products, per_device(): jnp.einsum('rk,ckm->crm', rounded, impedance[0, 0], preferred_element_typ...  3.9 us
    pallas_call x2, Pallas kernels, on_chip(): pl.pallas_call(kernel, in_specs=[full] * len(args), out_specs=[full] * le...  3.41 us
    pallas_call x1, Pallas kernels, solve_interfaces(): pl.pallas_call(interface_kernel, in_specs=[full] * len(args), out_specs=[...  2.71 us
  transfers between devices with their start and end apart: 12, of which 2 were waited for; matrix products, arithmetic and copies ran while one was open for 14% of the time, Pallas kernels for 4%

profile of v4, /device:TPU:0, one launch (start us, length us, event | category | flops | bytes accessed | tf_op | source)
XLA Modules:
  0.0 77.6 jit_solution(6507964030327085343)
XLA Ops:
  0.0 1.1 %bitcast_convert_fusion = bf16[2,64,1152]{2,1,0:T(8,128)(2,1)S(1)} fusion(f32[1,1,2,64,1152]{4,3,2,1,0:T(8,128)} %param.6), kind=kLoop, calls=%fused_computation.91 | loop fusion | flops 147456 | bytes 884736 | tf_op jit(solution)/shard_map/convert.7
  1.3 5.1 %collective-permute-start.1 = (bf16[2,64,192]{2,1,0:T(8,128)(2,1)S(1)}, bf16[2,64,192]{2,1,0:T(8,128)(2,1)S(1)}, u32[]{:S(2)}, u32[]{:S(2)}) collective-permute-start(bf16[2,64,192]{2,1,0:T(8,128)(2,1)S(1)} %get-tuple-element.61), channel_id=1, source_target_pairs={{0,24},{8,0},{16,8},{24,16},{1,25},{9,1},{17,9},{25,17},{2,26},{10... | collective-permute-start | bytes 147464 | tf_op jit(solution)/shard_map/ppermute | solution.py:15
  6.4 0.7 collective-permute-start
  7.2 0.6 fusion.39
  11.2 1.5 %collective-permute-start.4 = (f32[16,512]{1,0:T(8,128)S(1)}, f32[16,512]{1,0:T(8,128)S(1)}, u32[]{:S(2)}, u32[]{:S(2)}) collective-permute-start(f32[16,512]{1,0:T(8,128)S(1)} %copy-done.12), channel_id=1, source_target_pairs={{0,1},{1,0},{2,3},{3,2},{4,5},{5,4},{6,7},{7,6},{8,9},{9,8},{10,11... | collective-permute-start | bytes 98312 | tf_op jit(solution)/shard_map/ppermute | solution.py:44
  13.4 0.8 %maximum_select_fusion = bf16[384,384]{1,0:T(8,128)(2,1)} fusion(bf16[384,192]{1,0:T(8,128)(2,1)S(1)} %get-tuple-element.54, bf16[384,192]{1,0:T(8,128)(2,1)S(1)} %get-tuple-element.53, pred[]{:T(512)S(6)} %lt.25), kind=kLoop, calls=%fused_computation.27 | loop fusion | flops 737280 | bytes 589825 | tf_op jit(solution)/shard_map/jit(_where)/select_n | solution.py:233
  15.3 0.9 %maximum_select_fusion.2 = bf16[384,384]{1,0:T(8,128)(2,1)} fusion(bf16[384,192]{1,0:T(8,128)(2,1)S(1)} %get-tuple-element.50, bf16[384,192]{1,0:T(8,128)(2,1)S(1)} %get-tuple-element.49, pred[]{:T(512)S(6)} %lt.24), kind=kLoop, calls=%fused_computation.29 | loop fusion | flops 737280 | bytes 589825 | tf_op jit(solution)/shard_map/jit(_where)/select_n | solution.py:234
  16.2 1.1 %collective-permute-start.10 = (bf16[384,384]{1,0:T(8,128)(2,1)}, bf16[384,384]{1,0:T(8,128)(2,1)}, u32[]{:S(2)}, u32[]{:S(2)}) collective-permute-start(bf16[384,384]{1,0:T(8,128)(2,1)} %maximum_select_fusion.2), channel_id=1, source_target_pairs={{0,2},{2,4},{4,6},{6,0},{1,3},{3,5},{5,7},{7,1},{8,10},{10,12},{12... | collective-permute-start | bytes 884744 | tf_op jit(solution)/shard_map/ppermute | solution.py:15
  17.2 0.8 slice_bitcast_fusion.3
  18.0 0.8 %maximum_select_fusion.1.own_x = bf16[384,384]{1,0:T(8,128)(2,1)} fusion(bf16[384,192]{1,0:T(8,128)(2,1)S(1)} %get-tuple-element.52, bf16[384,192]{1,0:T(8,128)(2,1)S(1)} %get-tuple-element.51, pred[]{:T(512)S(6)} %lt.25), kind=kLoop, calls=%fused_computation.28 | loop fusion | flops 737280 | bytes 589825 | tf_op jit(solution)/shard_map/jit(_where)/select_n | solution.py:233
  19.5 1.4 %shard_map.64 = (f32[2,64,1152]{2,1,0:T(8,128)S(1)}, f32[16,16,128]{2,1,0:T(8,128)}, f32[1,64]{1,0:T(1,128)S(1)}) custom-call(f32[2,64,192]{2,1,0:T(8,128)S(1)} %collective-permute-done.2.zero, f32[2,64,192]{2,1,0:T(8,128)S(1)} %get-tuple-element.71.one, f32[2,64,192]{2,1,0:T(8,128)S(1)} %collective-permute-done.3.two, ...), custom_call_target="tpu_custom_call" | custom-call | flops 28311552 | bytes 786432 | tf_op jit(solution)/shard_map/pallas_call | solution.py:169
  20.9 5.0 %all-to-all-start = ((f32[16,16,128]{2,1,0:T(8,128)}), f32[16,16,128]{2,1,0:T(8,128)}, u32[]{:S(2)}, u32[]{:S(2)}) async-start(f32[16,16,128]{2,1,0:T(8,128)} %get-tuple-element.23), calls=%async_computation | async-start | bytes 262144 | tf_op jit(solution)/shard_map/all_to_all | solution.py:38
  26.0 3.9 %fusion.2.products = f32[2,192,1152]{2,1,0:T(8,128)S(1)} fusion(bf16[192,1152,1]{1,0,2:T(8,128)(2,1)S(1)} %bitcast.87, bf16[1,1,2,1152,1152]{4,3,2,1,0:T(8,128)(2,1)} %param.7), kind=kOutput, calls=%fused_computation.2 | convolution fusion | flops 1019215872 | bytes 7520256 | tf_op jit(solution)/shard_map/rk,ckm->crm/dot_general | solution.py:256
  29.9 3.9 %all-to-all-done.gathered = f32[16,16,128]{2,1,0:T(8,128)} async-done(((f32[16,16,128]{2,1,0:T(8,128)}), f32[16,16,128]{2,1,0:T(8,128)}, u32[]{:S(2)}, u32[]{:S(2)}) %all-to-all-start) | async-done | bytes 131104 | tf_op jit(solution)/shard_map/all_to_all | solution.py:38
  33.8 0.8 %copy-done.2 = f32[32,512]{1,0:T(8,128)S(1)} copy-done((f32[32,512]{1,0:T(8,128)S(1)}, f32[32,512]{1,0:T(8,128)}, u32[]{:S(2)}) %copy-start.2) | copy-done | bytes 65560
  34.6 2.1 %shard_map.65 = (f32[2,64,1152]{2,1,0:T(8,128)S(1)}, bf16[2,128,1152]{2,1,0:T(8,128)(2,1)S(1)}, f32[1,128]{1,0:T(1,128)S(1)}) custom-call(f32[16,16,128]{2,1,0:T(8,128)} %all-to-all-done.gathered, f32[32,512]{1,0:T(8,128)S(1)} %copy-done.2, f32[2,32,1152]{2,1,0:T(8,128)S(1)} %bitcast.86, f32[2,192,1152]{2,1,0:T(8,128)S(1)} %fusion.2.products, ...), custom_call_target="tpu_custom_call" | custom-call | flops 56623104 | bytes 2851072 | tf_op jit(solution)/shard_map/pallas_call | solution.py:169
  37.0 0.8 %collective-permute-start.5 = (bf16[2,128,192]{2,1,0:T(8,128)(2,1)S(1)}, bf16[2,128,192]{2,1,0:T(8,128)(2,1)S(1)}, u32[]{:S(2)}, u32[]{:S(2)}) collective-permute-start(bf16[2,128,192]{2,1,0:T(8,128)(2,1)S(1)} %get-tuple-element.45), channel_id=1, source_target_pairs={{0,0},{8,16},{16,8},{24,24},{1,1},{9,17},{17,9},{25,25},{2,2},{10,... | collective-permute-start | bytes 294920 | tf_op jit(solution)/shard_map/ppermute | solution.py:24
  38.0 3.9 %collective-permute-done.6 = bf16[2,128,192]{2,1,0:T(8,128)(2,1)S(1)} collective-permute-done((bf16[2,128,192]{2,1,0:T(8,128)(2,1)S(1)}, bf16[2,128,192]{2,1,0:T(8,128)(2,1)S(1)}, u32[]{:S(2)}, u32[]{:S(2)}) %collective-permute-start.6) | collective-permute-done | bytes 98336 | tf_op jit(solution)/shard_map/ppermute | solution.py:24
  41.9 0.7 collective-permute-start.7
  42.7 2.7 %interfaces.1 = (f32[2,128,1152]{2,1,0:T(8,128)S(1)}, f32[16,40,128]{2,1,0:T(8,128)S(1)}) custom-call(bf16[2,128,1152]{2,1,0:T(8,128)(2,1)S(1)} %get-tuple-element.27.out, bf16[2,128,192]{2,1,0:T(8,128)(2,1)S(1)} %get-tuple-element.68.low_x, bf16[2,128,192]{2,1,0:T(8,128)(2,1)S(1)} %get-tuple-element.67.high_x, ...), custom_call_target="tpu_custom_call" | custom-call | flops 452984832 | bytes 5898240 | tf_op jit(solution)/shard_map/interfaces/pallas_call | solution.py:183
  45.5 19.9 %all_to_all.15 = f32[16,40,128]{2,1,0:T(8,128)S(1)} all-to-all(f32[16,40,128]{2,1,0:T(8,128)S(1)} %get-tuple-element.32), channel_id=1, replica_groups=mesh['gx'=4,'gy'=4,'col'=2] {'gx','gy'}, dimensions={0} | all-to-all | bytes 655360 | tf_op jit(solution)/shard_map/all_to_all | solution.py:38
  66.0 0.8 multiply_reduce_fusion
  67.1 9.4 %all_to_all.16 = f32[16,1,128]{2,1,0:T(1,128)S(1)} all-to-all(f32[16,1,128]{2,1,0:T(1,128)S(1)} %broadcast_in_dim.18), channel_id=1, replica_groups=mesh['gx'=4,'gy'=4,'col'=2] {'gx','gy'}, dimensions={0} | all-to-all | bytes 16384 | tf_op jit(solution)/shard_map/all_to_all | solution.py:38
  76.6 1.0 %fusion.5 = f32[1,1,2,64,1152]{4,3,2,1,0:T(8,128)} fusion(f32[64,2,1152]{2,0,1:T(8,128)S(1)} %get-tuple-element.78, f32[64]{0:T(128)S(1)} %sqrt_multiply_fusion, f32[2,128,1152]{2,1,0:T(8,128)S(1)} %get-tuple-element.31, f32[64]{0:T(128)S(1)} %sqrt_multiply_fusion.1), kind=kLoop, calls=%fused_computation.9 | loop fusion | flops 589824 | bytes 2359808 | tf_op jit(solution)/shard_map/broadcast_in_dim | solution.py:286
  (81 shorter events, 6.1 us)
Async XLA Ops:
  0.0 7.1 %copy-start.3 = (f32[1,1,32,2,1152]{4,3,2,1,0:T(2,128)S(1)}, f32[1,1,32,2,1152]{4,3,2,1,0:T(2,128)}, u32[]{:S(2)}) copy-start(f32[1,1,32,2,1152]{4,3,2,1,0:T(2,128)} %param.10) | copy-start | bytes 884740
  1.1 6.1 %copy-start.13 = (s32[1,1,2]{2,1,0:T(1,128)S(1)}, s32[1,1,2]{2,1,0:T(1,128)}, u32[]{:S(2)}) copy-start(s32[1,1,2]{2,1,0:T(1,128)} %param.9) | copy-start | bytes 28
  1.3 8.0 %copy-start.5 = (bf16[1,1,2,2,384,384]{5,4,3,2,1,0:T(8,128)(2,1)S(1)}, bf16[1,1,2,2,384,384]{5,4,3,2,1,0:T(8,128)(2,1)}, u32[]{:S(2)}) copy-start(bf16[1,1,2,2,384,384]{5,4,3,2,1,0:T(8,128)(2,1)} %param.8) | copy-start | bytes 3538948
  1.3 8.0 %collective-permute-start.1 = (bf16[2,64,192]{2,1,0:T(8,128)(2,1)S(1)}, bf16[2,64,192]{2,1,0:T(8,128)(2,1)S(1)}, u32[]{:S(2)}, u32[]{:S(2)}) collective-permute-start(bf16[2,64,192]{2,1,0:T(8,128)(2,1)S(1)} %get-tuple-element.61), channel_id=1, source_target_pairs={{0,24},{8,0},{16,8},{24,16},{1,25},{9,1},{17,9},{25,17},{2,26},{10... | collective-permute-start | bytes 147464 | tf_op jit(solution)/shard_map/ppermute | solution.py:15
  6.4 3.4 %collective-permute-start = (bf16[2,64,192]{2,1,0:T(8,128)(2,1)S(1)}, bf16[2,64,192]{2,1,0:T(8,128)(2,1)S(1)}, u32[]{:S(2)}, u32[]{:S(2)}) collective-permute-start(bf16[2,64,192]{2,1,0:T(8,128)(2,1)S(1)} %get-tuple-element.63), channel_id=1, source_target_pairs={{0,6},{2,0},{4,2},{6,4},{1,7},{3,1},{5,3},{7,5},{8,14},{10,8},{12,... | collective-permute-start | bytes 147464 | tf_op jit(solution)/shard_map/ppermute | solution.py:15
  10.7 8.8 %collective-permute-start.2 = (f32[2,64,192]{2,1,0:T(8,128)S(1)}, f32[2,64,192]{2,1,0:T(8,128)S(1)}, u32[]{:S(2)}, u32[]{:S(2)}) collective-permute-start(f32[2,64,192]{2,1,0:T(8,128)S(1)} %get-tuple-element.19), channel_id=1, source_target_pairs={{0,8},{8,16},{16,24},{24,0},{1,9},{9,17},{17,25},{25,1},{2,10},{10... | collective-permute-start | bytes 294920 | tf_op jit(solution)/shard_map/ppermute | solution.py:15
  10.7 8.8 %collective-permute-start.3 = (f32[2,64,192]{2,1,0:T(8,128)S(1)}, f32[2,64,192]{2,1,0:T(8,128)S(1)}, u32[]{:S(2)}, u32[]{:S(2)}) collective-permute-start(f32[2,64,192]{2,1,0:T(8,128)S(1)} %get-tuple-element.20), channel_id=1, source_target_pairs={{0,2},{2,4},{4,6},{6,0},{1,3},{3,5},{5,7},{7,1},{8,10},{10,12},{12... | collective-permute-start | bytes 294920 | tf_op jit(solution)/shard_map/ppermute | solution.py:15
  11.2 7.6 %collective-permute-start.4 = (f32[16,512]{1,0:T(8,128)S(1)}, f32[16,512]{1,0:T(8,128)S(1)}, u32[]{:S(2)}, u32[]{:S(2)}) collective-permute-start(f32[16,512]{1,0:T(8,128)S(1)} %copy-done.12), channel_id=1, source_target_pairs={{0,1},{1,0},{2,3},{3,2},{4,5},{5,4},{6,7},{7,6},{8,9},{9,8},{10,11... | collective-permute-start | bytes 98312 | tf_op jit(solution)/shard_map/ppermute | solution.py:44
  14.2 28.5 %collective-permute-start.9 = (bf16[384,384]{1,0:T(8,128)(2,1)}, bf16[384,384]{1,0:T(8,128)(2,1)}, u32[]{:S(2)}, u32[]{:S(2)}) collective-permute-start(bf16[384,384]{1,0:T(8,128)(2,1)} %maximum_select_fusion), channel_id=1, source_target_pairs={{0,8},{8,16},{16,24},{24,0},{1,9},{9,17},{17,25},{25,1},{2,10},{10... | collective-permute-start | bytes 884744 | tf_op jit(solution)/shard_map/ppermute | solution.py:15
  16.2 26.5 %collective-permute-start.10 = (bf16[384,384]{1,0:T(8,128)(2,1)}, bf16[384,384]{1,0:T(8,128)(2,1)}, u32[]{:S(2)}, u32[]{:S(2)}) collective-permute-start(bf16[384,384]{1,0:T(8,128)(2,1)} %maximum_select_fusion.2), channel_id=1, source_target_pairs={{0,2},{2,4},{4,6},{6,0},{1,3},{3,5},{5,7},{7,1},{8,10},{10,12},{12... | collective-permute-start | bytes 884744 | tf_op jit(solution)/shard_map/ppermute | solution.py:15
  18.9 7.1 %copy-start.8 = (f32[16,512]{1,0:T(8,128)}, f32[16,512]{1,0:T(8,128)S(1)}, u32[]{:S(2)}) copy-start(f32[16,512]{1,0:T(8,128)S(1)} %get-tuple-element.73) | copy-start | bytes 98308
  18.9 7.1 %copy-start.10 = (f32[16,512]{1,0:T(8,128)}, f32[16,512]{1,0:T(8,128)S(1)}, u32[]{:S(2)}) copy-start(f32[16,512]{1,0:T(8,128)S(1)} %get-tuple-element.74) | copy-start | bytes 98308
  20.9 12.9 %all-to-all-start = ((f32[16,16,128]{2,1,0:T(8,128)}), f32[16,16,128]{2,1,0:T(8,128)}, u32[]{:S(2)}, u32[]{:S(2)}) async-start(f32[16,16,128]{2,1,0:T(8,128)} %get-tuple-element.23), calls=%async_computation | async-start | bytes 262144 | tf_op jit(solution)/shard_map/all_to_all | solution.py:38
  26.0 7.9 %copy-start = (f32[1,1,2,64,1152]{4,3,2,1,0:T(8,128)S(1)}, f32[1,1,2,64,1152]{4,3,2,1,0:T(8,128)}, u32[]{:S(2)}) copy-start(f32[1,1,2,64,1152]{4,3,2,1,0:T(8,128)} %param.6) | copy-start | bytes 1769476
  36.7 1.1 %copy-start.6 = (bf16[384,192]{1,0:T(8,128)(2,1)S(1)}, bf16[384,192]{1,0:T(8,128)(2,1)}, u32[]{:S(2)}) copy-start(bf16[384,192]{1,0:T(8,128)(2,1)} %get-tuple-element.47) | copy-start | bytes 442372
  36.7 1.1 %copy-start.7 = (bf16[384,192]{1,0:T(8,128)(2,1)S(1)}, bf16[384,192]{1,0:T(8,128)(2,1)}, u32[]{:S(2)}) copy-start(bf16[384,192]{1,0:T(8,128)(2,1)} %get-tuple-element.48) | copy-start | bytes 442372
  36.7 6.0 %copy-start.1 = (bf16[384,384]{1,0:T(8,128)(2,1)S(1)}, bf16[384,384]{1,0:T(8,128)(2,1)}, u32[]{:S(2)}) copy-start(bf16[384,384]{1,0:T(8,128)(2,1)} %maximum_select_fusion.1.own_x) | copy-start | bytes 884740
  36.9 5.0 %collective-permute-start.6 = (bf16[2,128,192]{2,1,0:T(8,128)(2,1)S(1)}, bf16[2,128,192]{2,1,0:T(8,128)(2,1)S(1)}, u32[]{:S(2)}, u32[]{:S(2)}) collective-permute-start(bf16[2,128,192]{2,1,0:T(8,128)(2,1)S(1)} %get-tuple-element.46), channel_id=1, source_target_pairs={{0,8},{8,0},{16,24},{24,16},{1,9},{9,1},{17,25},{25,17},{2,10},{10... | collective-permute-start | bytes 294920 | tf_op jit(solution)/shard_map/ppermute | solution.py:24
  37.0 5.6 %collective-permute-start.5 = (bf16[2,128,192]{2,1,0:T(8,128)(2,1)S(1)}, bf16[2,128,192]{2,1,0:T(8,128)(2,1)S(1)}, u32[]{:S(2)}, u32[]{:S(2)}) collective-permute-start(bf16[2,128,192]{2,1,0:T(8,128)(2,1)S(1)} %get-tuple-element.45), channel_id=1, source_target_pairs={{0,0},{8,16},{16,8},{24,24},{1,1},{9,17},{17,9},{25,25},{2,2},{10,... | collective-permute-start | bytes 294920 | tf_op jit(solution)/shard_map/ppermute | solution.py:24
  37.9 4.7 %collective-permute-start.8 = (bf16[2,128,192]{2,1,0:T(8,128)(2,1)S(1)}, bf16[2,128,192]{2,1,0:T(8,128)(2,1)S(1)}, u32[]{:S(2)}, u32[]{:S(2)}) collective-permute-start(bf16[2,128,192]{2,1,0:T(8,128)(2,1)S(1)} %get-tuple-element.43), channel_id=1, source_target_pairs={{0,2},{2,0},{4,6},{6,4},{1,3},{3,1},{5,7},{7,5},{8,10},{10,8},{12,... | collective-permute-start | bytes 294920 | tf_op jit(solution)/shard_map/ppermute | solution.py:24
  41.9 0.7 collective-permute-start.7
  45.4 20.2 %copy-start.9 = (f32[16,512]{1,0:T(8,128)S(1)}, f32[16,512]{1,0:T(8,128)}, u32[]{:S(2)}) copy-start(f32[16,512]{1,0:T(8,128)} %copy-done.8) | copy-start | bytes 98308
  45.4 20.2 %copy-start.11 = (f32[16,512]{1,0:T(8,128)S(1)}, f32[16,512]{1,0:T(8,128)}, u32[]{:S(2)}) copy-start(f32[16,512]{1,0:T(8,128)} %copy-done.10) | copy-start | bytes 98308
  45.5 20.5 %copy-start.4 = (f32[1,1,32,2,1152]{4,3,2,1,0:T(2,128)S(1)}, f32[1,1,32,2,1152]{4,3,2,1,0:T(2,128)}, u32[]{:S(2)}) copy-start(f32[1,1,32,2,1152]{4,3,2,1,0:T(2,128)} %param.10) | copy-start | bytes 884740
  (2 other events, 1.6 us)

commit v5 on v4

--- a/solution.py
+++ b/solution.py
@@ -38,12 +38,17 @@
     return lax.all_to_all(copies, GRID, 0, 0, tiled=True)
 
 
-def both_halves(rows):
+def halves_of_rows(rows):
     if lax.axis_size("col") != 2:
-        return lax.all_gather(rows, "col", axis=0, tiled=True)
-    other = lax.ppermute(rows, "col", [(0, 1), (1, 0)])
+        return lax.all_gather(rows, "col", axis=0, tiled=True), None
+    return rows, lax.ppermute(rows, "col", [(0, 1), (1, 0)])
+
+
+def in_order(mine, other):
+    if other is None:
+        return mine
     mine_first = lax.axis_index("col") == 0
-    return jnp.concatenate([jnp.where(mine_first, rows, other), jnp.where(mine_first, other, rows)])
+    return jnp.concatenate([jnp.where(mine_first, mine, other), jnp.where(mine_first, other, mine)])
 
 
 def halves(solver, leading, face_width):
@@ -248,12 +253,14 @@
     )
     payload, state = lax.optimization_barrier((payload, updated))
     gathered = spread(payload)
-    rows = both_halves(part_rows)
+    mine, other = halves_of_rows(part_rows)
 
     rounded = jnp.concatenate([state, basis_first], axis=1).astype(jnp.bfloat16)
     total = count + coarse_count
     rounded = rounded.reshape(2 * total, -1)
     products = jnp.einsum("rk,ckm->crm", rounded, impedance[0, 0], preferred_element_type=jnp.float32)
+    products, mine, other = lax.optimization_barrier((products, mine, other))
+    rows = in_order(mine, other)
     correction, outgoing, sums = on_chip(
         correct_kernel,
         [

time: 78.1 us -> 78.6 us (level)
  waiting for transfers between devices: 7.87 us -> 5.15 us
  blocking collectives: 29.3 us -> 30.5 us
  starting transfers between devices: 15.7 us -> 16.7 us
  other arithmetic: 7.64 us -> 8.43 us
    all_to_all x1, waiting for transfers between devices: 3.93 us -> 1.9 us  [spread(): return lax.all_to_all(copies, GRID, 0, 0, tiled=True)]
    all_to_all x2, blocking collectives: 29.3 us -> 30.5 us  [spread(): return lax.all_to_all(copies, GRID, 0, 0, tiled=True)]
  transfers between devices with their start and end apart: 12 -> 12, of which waited for: 2 -> 2; matrix products, arithmetic and copies ran while one was open for 14% -> 15% of each run, Pallas kernels for 4% -> 4%
where the time goes in v5:
time: 78.6 us; the launch traced here: 78.2 us
  blocking collectives  30.5 us (39%)
  starting transfers between devices  16.7 us (21%)
  other arithmetic  8.43 us (11%)
  Pallas kernels  6.13 us (8%)
  matrix products  6.03 us (8%)
  waiting for transfers between devices  5.15 us (7%)
  local copies, waits for them, and re-layouts  3.41 us (4%)
  between operations  1.8 us (2%)
    all_to_all x2, blocking collectives, spread(): return lax.all_to_all(copies, GRID, 0, 0, tiled=True)  30.5 us
    ppermute x6, starting transfers between devices, shifted(): lax.ppermute(block, axis, [(i, (i + distance) % count) for i in range(cou...  7.91 us
    all_to_all x1, starting transfers between devices, spread(): return lax.all_to_all(copies, GRID, 0, 0, tiled=True)  4.97 us
    dot_general x1, matrix products, per_device(): jnp.einsum('rk,ckm->crm', rounded, impedance[0, 0], preferred_element_typ...  3.9 us
    pallas_call x2, Pallas kernels, on_chip(): pl.pallas_call(kernel, in_specs=[full] * len(args), out_specs=[full] * le...  3.41 us
    ppermute x4, waiting for transfers between devices, swap(): return lax.ppermute(mine, axis, list(enumerate(partner)))  3.23 us
    pallas_call x1, Pallas kernels, solve_interfaces(): pl.pallas_call(interface_kernel, in_specs=[full] * len(args), out_specs=[...  2.72 us
    ppermute x4, starting transfers between devices, swap(): return lax.ppermute(mine, axis, list(enumerate(partner)))  2.3 us
  transfers between devices with their start and end apart: 12, of which 2 were waited for; matrix products, arithmetic and copies ran while one was open for 15% of the time, Pallas kernels for 4%

profile of v5, /device:TPU:0, one launch (start us, length us, event | category | flops | bytes accessed | tf_op | source)
XLA Modules:
  0.0 78.2 jit_solution(15977860957006323876)
XLA Ops:
  0.0 1.1 %bitcast_convert_fusion = bf16[2,64,1152]{2,1,0:T(8,128)(2,1)S(1)} fusion(f32[1,1,2,64,1152]{4,3,2,1,0:T(8,128)} %param.6), kind=kLoop, calls=%fused_computation.91 | loop fusion | flops 147456 | bytes 884736 | tf_op jit(solution)/shard_map/convert.7
  1.3 5.1 %collective-permute-start.1 = (bf16[2,64,192]{2,1,0:T(8,128)(2,1)S(1)}, bf16[2,64,192]{2,1,0:T(8,128)(2,1)S(1)}, u32[]{:S(2)}, u32[]{:S(2)}) collective-permute-start(bf16[2,64,192]{2,1,0:T(8,128)(2,1)S(1)} %get-tuple-element.67), channel_id=1, source_target_pairs={{0,24},{8,0},{16,8},{24,16},{1,25},{9,1},{17,9},{25,17},{2,26},{10... | collective-permute-start | bytes 147464 | tf_op jit(solution)/shard_map/ppermute | solution.py:15
  6.4 0.7 collective-permute-start
  11.0 1.5 %collective-permute-start.4 = (f32[16,512]{1,0:T(8,128)}, f32[16,512]{1,0:T(8,128)}, u32[]{:S(2)}, u32[]{:S(2)}) collective-permute-start(f32[16,512]{1,0:T(8,128)} %param.11), channel_id=1, source_target_pairs={{0,1},{1,0},{2,3},{3,2},{4,5},{5,4},{6,7},{7,6},{8,9},{9,8},{10,11... | collective-permute-start | bytes 98312 | tf_op jit(solution)/shard_map/ppermute | solution.py:44
  13.1 0.8 %maximum_select_fusion = bf16[384,384]{1,0:T(8,128)(2,1)} fusion(bf16[384,192]{1,0:T(8,128)(2,1)S(1)} %get-tuple-element.60, bf16[384,192]{1,0:T(8,128)(2,1)S(1)} %get-tuple-element.59, pred[]{:T(512)S(6)} %lt.25), kind=kLoop, calls=%fused_computation.27 | loop fusion | flops 737280 | bytes 589825 | tf_op jit(solution)/shard_map/jit(_where)/select_n | solution.py:238
  14.0 0.7 collective-permute-start.9
  15.3 0.8 %maximum_select_fusion.2 = bf16[384,384]{1,0:T(8,128)(2,1)} fusion(bf16[384,192]{1,0:T(8,128)(2,1)S(1)} %get-tuple-element.56, bf16[384,192]{1,0:T(8,128)(2,1)S(1)} %get-tuple-element.55, pred[]{:T(512)S(6)} %lt.24), kind=kLoop, calls=%fused_computation.29 | loop fusion | flops 737280 | bytes 589825 | tf_op jit(solution)/shard_map/jit(_where)/select_n | solution.py:239
  16.1 1.1 %collective-permute-start.10 = (bf16[384,384]{1,0:T(8,128)(2,1)}, bf16[384,384]{1,0:T(8,128)(2,1)}, u32[]{:S(2)}, u32[]{:S(2)}) collective-permute-start(bf16[384,384]{1,0:T(8,128)(2,1)} %maximum_select_fusion.2), channel_id=1, source_target_pairs={{0,2},{2,4},{4,6},{6,0},{1,3},{3,5},{5,7},{7,1},{8,10},{10,12},{12... | collective-permute-start | bytes 884744 | tf_op jit(solution)/shard_map/ppermute | solution.py:15
  17.2 0.8 slice_bitcast_fusion.3
  18.0 0.9 %maximum_select_fusion.1.own_x = bf16[384,384]{1,0:T(8,128)(2,1)} fusion(bf16[384,192]{1,0:T(8,128)(2,1)S(1)} %get-tuple-element.58, bf16[384,192]{1,0:T(8,128)(2,1)S(1)} %get-tuple-element.57, pred[]{:T(512)S(6)} %lt.25), kind=kLoop, calls=%fused_computation.28 | loop fusion | flops 737280 | bytes 589825 | tf_op jit(solution)/shard_map/jit(_where)/select_n | solution.py:238
  18.8 1.4 %shard_map.64 = (f32[2,64,1152]{2,1,0:T(8,128)S(1)}, f32[16,16,128]{2,1,0:T(8,128)}, f32[1,64]{1,0:T(1,128)S(1)}) custom-call(f32[2,64,192]{2,1,0:T(8,128)S(1)} %collective-permute-done.2.zero, f32[2,64,192]{2,1,0:T(8,128)S(1)} %get-tuple-element.77.one, f32[2,64,192]{2,1,0:T(8,128)S(1)} %collective-permute-done.3.two, ...), custom_call_target="tpu_custom_call" | custom-call | flops 28311552 | bytes 786432 | tf_op jit(solution)/shard_map/pallas_call | solution.py:174
  20.2 5.0 %all-to-all-start = ((f32[16,16,128]{2,1,0:T(8,128)}), f32[16,16,128]{2,1,0:T(8,128)}, u32[]{:S(2)}, u32[]{:S(2)}) async-start(f32[16,16,128]{2,1,0:T(8,128)} %get-tuple-element.26), calls=%async_computation | async-start | bytes 262144 | tf_op jit(solution)/shard_map/all_to_all | solution.py:38
  25.3 3.9 %fusion.2.products = f32[2,192,1152]{2,1,0:T(8,128)S(1)} fusion(bf16[192,1152,1]{1,0,2:T(8,128)(2,1)S(1)} %bitcast.87, bf16[1,1,2,1152,1152]{4,3,2,1,0:T(8,128)(2,1)} %param.7), kind=kOutput, calls=%fused_computation.2 | convolution fusion | flops 1019215872 | bytes 7520256 | tf_op jit(solution)/shard_map/rk,ckm->crm/dot_general | solution.py:261
  29.2 0.8 %broadcast_select_fusion.9 = (f32[16,512]{1,0:T(8,128)S(1)}, f32[16,512]{1,0:T(8,128)S(1)}) fusion(f32[16,512]{1,0:T(8,128)} %param.11, f32[16,512]{1,0:T(8,128)} %collective-permute-done.4, pred[]{:T(512)S(6)} %eq.44), kind=kLoop, calls=%fused_computation.80 | loop fusion | flops 16384 | bytes 131073 | tf_op jit(solution)/shard_map/jit(_where)/select_n | solution.py:51
  31.2 1.9 %all-to-all-done.gathered = f32[16,16,128]{2,1,0:T(8,128)} async-done(((f32[16,16,128]{2,1,0:T(8,128)}), f32[16,16,128]{2,1,0:T(8,128)}, u32[]{:S(2)}, u32[]{:S(2)}) %all-to-all-start) | async-done | bytes 131104 | tf_op jit(solution)/shard_map/all_to_all | solution.py:38
  33.1 0.8 %copy-done.2 = f32[32,512]{1,0:T(8,128)S(1)} copy-done((f32[32,512]{1,0:T(8,128)S(1)}, f32[32,512]{1,0:T(8,128)}, u32[]{:S(2)}) %copy-start.2) | copy-done | bytes 65560
  34.0 2.1 %shard_map.65 = (f32[2,64,1152]{2,1,0:T(8,128)S(1)}, bf16[2,128,1152]{2,1,0:T(8,128)(2,1)S(1)}, f32[1,128]{1,0:T(1,128)S(1)}) custom-call(f32[16,16,128]{2,1,0:T(8,128)} %all-to-all-done.gathered, f32[32,512]{1,0:T(8,128)S(1)} %copy-done.2, f32[2,32,1152]{2,1,0:T(8,128)S(1)} %bitcast.86, f32[2,192,1152]{2,1,0:T(8,128)S(1)} %fusion.2.products, ...), custom_call_target="tpu_custom_call" | custom-call | flops 56623104 | bytes 2851072 | tf_op jit(solution)/shard_map/pallas_call | solution.py:174
  38.0 3.2 %collective-permute-done.6 = bf16[2,128,192]{2,1,0:T(8,128)(2,1)S(1)} collective-permute-done((bf16[2,128,192]{2,1,0:T(8,128)(2,1)S(1)}, bf16[2,128,192]{2,1,0:T(8,128)(2,1)S(1)}, u32[]{:S(2)}, u32[]{:S(2)}) %collective-permute-start.6) | collective-permute-done | bytes 98336 | tf_op jit(solution)/shard_map/ppermute | solution.py:24
  41.2 0.7 collective-permute-start.7
  42.0 2.7 %interfaces.1 = (f32[2,128,1152]{2,1,0:T(8,128)S(1)}, f32[16,40,128]{2,1,0:T(8,128)S(1)}) custom-call(bf16[2,128,1152]{2,1,0:T(8,128)(2,1)S(1)} %get-tuple-element.33.out, bf16[2,128,192]{2,1,0:T(8,128)(2,1)S(1)} %get-tuple-element.74.low_x, bf16[2,128,192]{2,1,0:T(8,128)(2,1)S(1)} %get-tuple-element.73.high_x, ...), custom_call_target="tpu_custom_call" | custom-call | flops 452984832 | bytes 5898240 | tf_op jit(solution)/shard_map/interfaces/pallas_call | solution.py:188
  44.8 21.2 %all_to_all.15 = f32[16,40,128]{2,1,0:T(8,128)S(1)} all-to-all(f32[16,40,128]{2,1,0:T(8,128)S(1)} %get-tuple-element.38), channel_id=1, replica_groups=mesh['gx'=4,'gy'=4,'col'=2] {'gx','gy'}, dimensions={0} | all-to-all | bytes 655360 | tf_op jit(solution)/shard_map/all_to_all | solution.py:38
  66.5 0.8 multiply_reduce_fusion
  67.7 9.4 %all_to_all.16 = f32[16,1,128]{2,1,0:T(1,128)S(1)} all-to-all(f32[16,1,128]{2,1,0:T(1,128)S(1)} %broadcast_in_dim.18), channel_id=1, replica_groups=mesh['gx'=4,'gy'=4,'col'=2] {'gx','gy'}, dimensions={0} | all-to-all | bytes 16384 | tf_op jit(solution)/shard_map/all_to_all | solution.py:38
  77.2 1.0 %fusion.5 = f32[1,1,2,64,1152]{4,3,2,1,0:T(8,128)} fusion(f32[64,2,1152]{2,0,1:T(8,128)S(1)} %get-tuple-element.84, f32[64]{0:T(128)S(1)} %sqrt_multiply_fusion, f32[2,128,1152]{2,1,0:T(8,128)S(1)} %get-tuple-element.37, f32[64]{0:T(128)S(1)} %sqrt_multiply_fusion.1), kind=kLoop, calls=%fused_computation.9 | loop fusion | flops 589824 | bytes 2359808 | tf_op jit(solution)/shard_map/broadcast_in_dim | solution.py:293
  (79 shorter events, 8.1 us)
Async XLA Ops:
  0.0 7.1 %copy-start.3 = (f32[1,1,32,2,1152]{4,3,2,1,0:T(2,128)S(1)}, f32[1,1,32,2,1152]{4,3,2,1,0:T(2,128)}, u32[]{:S(2)}) copy-start(f32[1,1,32,2,1152]{4,3,2,1,0:T(2,128)} %param.10) | copy-start | bytes 884740
  1.1 6.1 %copy-start.12 = (s32[1,1,2]{2,1,0:T(1,128)S(1)}, s32[1,1,2]{2,1,0:T(1,128)}, u32[]{:S(2)}) copy-start(s32[1,1,2]{2,1,0:T(1,128)} %param.9) | copy-start | bytes 28
  1.3 8.0 %copy-start.5 = (bf16[1,1,2,2,384,384]{5,4,3,2,1,0:T(8,128)(2,1)S(1)}, bf16[1,1,2,2,384,384]{5,4,3,2,1,0:T(8,128)(2,1)}, u32[]{:S(2)}) copy-start(bf16[1,1,2,2,384,384]{5,4,3,2,1,0:T(8,128)(2,1)} %param.8) | copy-start | bytes 3538948
  1.3 8.0 %collective-permute-start.1 = (bf16[2,64,192]{2,1,0:T(8,128)(2,1)S(1)}, bf16[2,64,192]{2,1,0:T(8,128)(2,1)S(1)}, u32[]{:S(2)}, u32[]{:S(2)}) collective-permute-start(bf16[2,64,192]{2,1,0:T(8,128)(2,1)S(1)} %get-tuple-element.67), channel_id=1, source_target_pairs={{0,24},{8,0},{16,8},{24,16},{1,25},{9,1},{17,9},{25,17},{2,26},{10... | collective-permute-start | bytes 147464 | tf_op jit(solution)/shard_map/ppermute | solution.py:15
  6.4 3.4 %collective-permute-start = (bf16[2,64,192]{2,1,0:T(8,128)(2,1)S(1)}, bf16[2,64,192]{2,1,0:T(8,128)(2,1)S(1)}, u32[]{:S(2)}, u32[]{:S(2)}) collective-permute-start(bf16[2,64,192]{2,1,0:T(8,128)(2,1)S(1)} %get-tuple-element.69), channel_id=1, source_target_pairs={{0,6},{2,0},{4,2},{6,4},{1,7},{3,1},{5,3},{7,5},{8,14},{10,8},{12,... | collective-permute-start | bytes 147464 | tf_op jit(solution)/shard_map/ppermute | solution.py:15
  10.7 8.2 %collective-permute-start.2 = (f32[2,64,192]{2,1,0:T(8,128)S(1)}, f32[2,64,192]{2,1,0:T(8,128)S(1)}, u32[]{:S(2)}, u32[]{:S(2)}) collective-permute-start(f32[2,64,192]{2,1,0:T(8,128)S(1)} %get-tuple-element.22), channel_id=1, source_target_pairs={{0,8},{8,16},{16,24},{24,0},{1,9},{9,17},{17,25},{25,1},{2,10},{10... | collective-permute-start | bytes 294920 | tf_op jit(solution)/shard_map/ppermute | solution.py:15
  10.7 8.1 %collective-permute-start.3 = (f32[2,64,192]{2,1,0:T(8,128)S(1)}, f32[2,64,192]{2,1,0:T(8,128)S(1)}, u32[]{:S(2)}, u32[]{:S(2)}) collective-permute-start(f32[2,64,192]{2,1,0:T(8,128)S(1)} %get-tuple-element.23), channel_id=1, source_target_pairs={{0,2},{2,4},{4,6},{6,0},{1,3},{3,5},{5,7},{7,1},{8,10},{10,12},{12... | collective-permute-start | bytes 294920 | tf_op jit(solution)/shard_map/ppermute | solution.py:15
  11.0 18.2 %collective-permute-start.4 = (f32[16,512]{1,0:T(8,128)}, f32[16,512]{1,0:T(8,128)}, u32[]{:S(2)}, u32[]{:S(2)}) collective-permute-start(f32[16,512]{1,0:T(8,128)} %param.11), channel_id=1, source_target_pairs={{0,1},{1,0},{2,3},{3,2},{4,5},{5,4},{6,7},{7,6},{8,9},{9,8},{10,11... | collective-permute-start | bytes 98312 | tf_op jit(solution)/shard_map/ppermute | solution.py:44
  14.0 28.0 %collective-permute-start.9 = (bf16[384,384]{1,0:T(8,128)(2,1)}, bf16[384,384]{1,0:T(8,128)(2,1)}, u32[]{:S(2)}, u32[]{:S(2)}) collective-permute-start(bf16[384,384]{1,0:T(8,128)(2,1)} %maximum_select_fusion), channel_id=1, source_target_pairs={{0,8},{8,16},{16,24},{24,0},{1,9},{9,17},{17,25},{25,1},{2,10},{10... | collective-permute-start | bytes 884744 | tf_op jit(solution)/shard_map/ppermute | solution.py:15
  16.1 25.9 %collective-permute-start.10 = (bf16[384,384]{1,0:T(8,128)(2,1)}, bf16[384,384]{1,0:T(8,128)(2,1)}, u32[]{:S(2)}, u32[]{:S(2)}) collective-permute-start(bf16[384,384]{1,0:T(8,128)(2,1)} %maximum_select_fusion.2), channel_id=1, source_target_pairs={{0,2},{2,4},{4,6},{6,0},{1,3},{3,5},{5,7},{7,1},{8,10},{10,12},{12... | collective-permute-start | bytes 884744 | tf_op jit(solution)/shard_map/ppermute | solution.py:15
  20.2 12.9 %all-to-all-start = ((f32[16,16,128]{2,1,0:T(8,128)}), f32[16,16,128]{2,1,0:T(8,128)}, u32[]{:S(2)}, u32[]{:S(2)}) async-start(f32[16,16,128]{2,1,0:T(8,128)} %get-tuple-element.26), calls=%async_computation | async-start | bytes 262144 | tf_op jit(solution)/shard_map/all_to_all | solution.py:38
  25.3 7.9 %copy-start = (f32[1,1,2,64,1152]{4,3,2,1,0:T(8,128)S(1)}, f32[1,1,2,64,1152]{4,3,2,1,0:T(8,128)}, u32[]{:S(2)}) copy-start(f32[1,1,2,64,1152]{4,3,2,1,0:T(8,128)} %param.6) | copy-start | bytes 1769476
  30.0 0.6 copy-start.10
  33.1 0.8 %copy-start.2 = (f32[32,512]{1,0:T(8,128)S(1)}, f32[32,512]{1,0:T(8,128)}, u32[]{:S(2)}) copy-start(f32[32,512]{1,0:T(8,128)} %pad_maximum_fusion.4.rows) | copy-start | bytes 196612
  36.0 1.5 %copy-start.6 = (bf16[384,192]{1,0:T(8,128)(2,1)S(1)}, bf16[384,192]{1,0:T(8,128)(2,1)}, u32[]{:S(2)}) copy-start(bf16[384,192]{1,0:T(8,128)(2,1)} %get-tuple-element.53) | copy-start | bytes 442372
  36.0 1.5 %copy-start.7 = (bf16[384,192]{1,0:T(8,128)(2,1)S(1)}, bf16[384,192]{1,0:T(8,128)(2,1)}, u32[]{:S(2)}) copy-start(bf16[384,192]{1,0:T(8,128)(2,1)} %get-tuple-element.54) | copy-start | bytes 442372
  36.0 6.0 %copy-start.1 = (bf16[384,384]{1,0:T(8,128)(2,1)S(1)}, bf16[384,384]{1,0:T(8,128)(2,1)}, u32[]{:S(2)}) copy-start(bf16[384,384]{1,0:T(8,128)(2,1)} %maximum_select_fusion.1.own_x) | copy-start | bytes 884740
  36.2 5.0 %collective-permute-start.6 = (bf16[2,128,192]{2,1,0:T(8,128)(2,1)S(1)}, bf16[2,128,192]{2,1,0:T(8,128)(2,1)S(1)}, u32[]{:S(2)}, u32[]{:S(2)}) collective-permute-start(bf16[2,128,192]{2,1,0:T(8,128)(2,1)S(1)} %get-tuple-element.52), channel_id=1, source_target_pairs={{0,8},{8,0},{16,24},{24,16},{1,9},{9,1},{17,25},{25,17},{2,10},{10... | collective-permute-start | bytes 294920 | tf_op jit(solution)/shard_map/ppermute | solution.py:24
  36.8 5.1 %collective-permute-start.5 = (bf16[2,128,192]{2,1,0:T(8,128)(2,1)S(1)}, bf16[2,128,192]{2,1,0:T(8,128)(2,1)S(1)}, u32[]{:S(2)}, u32[]{:S(2)}) collective-permute-start(bf16[2,128,192]{2,1,0:T(8,128)(2,1)S(1)} %get-tuple-element.51), channel_id=1, source_target_pairs={{0,0},{8,16},{16,8},{24,24},{1,1},{9,17},{17,9},{25,25},{2,2},{10,... | collective-permute-start | bytes 294920 | tf_op jit(solution)/shard_map/ppermute | solution.py:24
  37.7 4.3 %collective-permute-start.8 = (bf16[2,128,192]{2,1,0:T(8,128)(2,1)S(1)}, bf16[2,128,192]{2,1,0:T(8,128)(2,1)S(1)}, u32[]{:S(2)}, u32[]{:S(2)}) collective-permute-start(bf16[2,128,192]{2,1,0:T(8,128)(2,1)S(1)} %get-tuple-element.49), channel_id=1, source_target_pairs={{0,2},{2,0},{4,6},{6,4},{1,3},{3,1},{5,7},{7,5},{8,10},{10,8},{12,... | collective-permute-start | bytes 294920 | tf_op jit(solution)/shard_map/ppermute | solution.py:24
  41.2 0.7 collective-permute-start.7
  44.8 21.4 %copy-start.9 = (f32[16,512]{1,0:T(8,128)S(1)}, f32[16,512]{1,0:T(8,128)}, u32[]{:S(2)}) copy-start(f32[16,512]{1,0:T(8,128)} %copy-done.8) | copy-start | bytes 98308
  44.8 21.4 %copy-start.11 = (f32[16,512]{1,0:T(8,128)S(1)}, f32[16,512]{1,0:T(8,128)}, u32[]{:S(2)}) copy-start(f32[16,512]{1,0:T(8,128)} %copy-done.10) | copy-start | bytes 98308
  44.8 21.7 %copy-start.4 = (f32[1,1,32,2,1152]{4,3,2,1,0:T(2,128)S(1)}, f32[1,1,32,2,1152]{4,3,2,1,0:T(2,128)}, u32[]{:S(2)}) copy-start(f32[1,1,32,2,1152]{4,3,2,1,0:T(2,128)} %param.10) | copy-start | bytes 884740
  (1 other events, 0.6 us)
